TPU v7x, 32 devices: a whole 2x2x4 slice. The times are simulated.
32 devices in a mesh: ctx: 8 (over z, y), tp: 4 (over x, core).
Axes of the slice: x: 2, y: 2, z: 4, core: 2. Of those that a mesh axis runs over, the one named last changes fastest.
Arguments:
- qkv: bfloat16 [1024, 3, 8192], P(('ctx', 'tp')), may hold values from -6 to 6
- filters: float32 [3, 7, 8192], P(None, None, 'tp'), may hold values from -1.5 to 1.5
- doc_ids: int32 [8], replicated, may hold values from 0 to 1, never falling along the last dimension, each value on 1 to 5 neighbouring positions
- upstream: bfloat16 [1024, 8192], P('ctx', 'tp'), may hold values from -6 to 6
Outputs:
- attended: bfloat16 [1024, 8192], P('ctx', 'tp')
- qkv_grad: bfloat16 [1024, 3, 8192], P(('ctx', 'tp'))
- filter_grad: float32 [3, 7, 8192], P(None, None, 'tp')
Inputs may be any that keep to these rules, and one draw needn't show every extreme that they name: doc_ids never falls along the sequence; every document covers 1 to 5 whole blocks of 128 tokens.
All inputs are finite; a program needn't handle non-finite values.
Results may differ from a plain program's by a relative error of at most 0.014.
The roundings to bfloat16 on the way count: a program that leaves them out, or rounds other values in their place, can miss the bound.
Values may be sent and summed in bfloat16 or wider, within the bound.
No kernel may reach another device: no remote copies, remote signals or barrier semaphores. Data moves between devices by JAX's collectives and lax.ppermute only.
A program may use at most 128 MiB of HBM per device.

v0:
```python
import jax
import jax.numpy as jnp
from jax import lax
from jax.sharding import PartitionSpec as P

HEAD_DIM = 128
KW = 7
BLOCK = 128
STEPS = 4


def from_behind(value, axis, steps):
    count = lax.axis_size(axis)
    first, last = (max(0, -steps), min(count, count - steps))
    return lax.ppermute(value, axis, [(source, source + steps) for source in range(first, last)])


def block_docs(doc_ids, first_block, count):
    start = jnp.maximum(first_block, 0)
    picked = lax.dynamic_slice_in_dim(doc_ids, start, count)
    return jnp.repeat(picked, BLOCK)


def shards(qkv, filters, doc_ids, upstream):
    local = lax.all_to_all(qkv, "tp", split_axis=2, concat_axis=0, tiled=True)
    tokens = local.shape[0]
    width = local.shape[2]
    heads = width // HEAD_DIM
    blocks_here = tokens // BLOCK
    logit_scale = HEAD_DIM ** (-0.5)
    position = lax.axis_index("ctx")
    reach = STEPS + 1
    rim = from_behind(local[tokens - (KW - 1) :], "ctx", 1)
    inputs = jnp.concatenate([rim, local], axis=0).astype(jnp.float32)
    mixed = sum(
        (filters[:, lag, :] * inputs[KW - 1 - lag : KW - 1 - lag + tokens] for lag in range(KW))
    )
    mixed = mixed.astype(jnp.bfloat16)
    queries = mixed[:, 0].reshape(tokens, heads, HEAD_DIM)
    key_value = mixed[:, 1:3]
    tiles = [key_value]
    current = key_value
    for distance in range(1, STEPS + 1):
        current = from_behind(current, "ctx", 1)
        tiles.append(current)
    joined = jnp.concatenate(tiles, axis=0)
    keys = joined[:, 0].reshape(reach * tokens, heads, HEAD_DIM)
    values = joined[:, 1].reshape(reach * tokens, heads, HEAD_DIM)
    rows = jnp.arange(tokens)
    query_token = position * tokens + rows
    query_doc = block_docs(doc_ids, position * blocks_here, blocks_here)
    key_tokens = jnp.concatenate(
        [(position - distance) * tokens + rows for distance in range(reach)]
    )
    key_docs = jnp.concatenate(
        [
            block_docs(doc_ids, (position - distance) * blocks_here, blocks_here)
            for distance in range(reach)
        ]
    )
    allowed = (
        (key_tokens[None, :] >= 0)
        & (key_tokens[None, :] <= query_token[:, None])
        & (key_docs[None, :] == query_doc[:, None])
    )
    raw = (
        jnp.einsum("qhd,khd->hqk", queries, keys, preferred_element_type=jnp.float32) * logit_scale
    )
    masked = jnp.where(allowed[None], raw, -1e30)
    row_max = masked.max(axis=2)
    expo = jnp.where(allowed[None], jnp.exp(masked - row_max[:, :, None]), 0.0)
    row_sum = expo.sum(axis=2)
    weighted_values = jnp.einsum(
        "hqk,khd->qhd", expo.astype(jnp.bfloat16), values, preferred_element_type=jnp.float32
    )
    attended = (weighted_values / row_sum.T[:, :, None]).astype(jnp.bfloat16)
    grad_out = upstream.reshape(tokens, heads, HEAD_DIM)
    delta = jnp.sum(grad_out.astype(jnp.float32) * attended.astype(jnp.float32), axis=-1).T
    prob = expo / row_sum[:, :, None]
    value_part = jnp.einsum(
        "hqk,qhd->khd", prob.astype(jnp.bfloat16), grad_out, preferred_element_type=jnp.float32
    )
    probability_gradient = jnp.einsum(
        "qhd,khd->hqk", grad_out, values, preferred_element_type=jnp.float32
    )
    score_gradient = (prob * (probability_gradient - delta[:, :, None]) * logit_scale).astype(
        jnp.bfloat16
    )
    query_gradient_rows = jnp.einsum(
        "hqk,khd->qhd", score_gradient, keys, preferred_element_type=jnp.float32
    )
    key_part = jnp.einsum(
        "hqk,qhd->khd", score_gradient, queries, preferred_element_type=jnp.float32
    )
    stacked = jnp.stack(
        [key_part.reshape(reach, tokens, width), value_part.reshape(reach, tokens, width)], axis=2
    )
    partials = [stacked[distance] for distance in range(reach)]
    carried = partials[STEPS]
    for distance in range(STEPS - 1, -1, -1):
        carried = from_behind(carried, "ctx", -1)
        carried = carried + partials[distance]
    conv_grad = jnp.concatenate([query_gradient_rows.reshape(tokens, 1, width), carried], axis=1)
    grad_edge = from_behind(conv_grad[: KW - 1], "ctx", -1)
    extended = jnp.concatenate([conv_grad, grad_edge], axis=0)
    input_grad = sum((filters[:, lag, :] * extended[lag : lag + tokens] for lag in range(KW)))
    tap_terms = jnp.stack(
        [
            jnp.sum(inputs[KW - 1 - lag : KW - 1 - lag + tokens] * conv_grad, axis=0)
            for lag in range(KW)
        ],
        axis=1,
    )
    filter_grad = lax.psum(tap_terms, "ctx")
    qkv_grad = lax.all_to_all(
        input_grad.astype(jnp.bfloat16), "tp", split_axis=0, concat_axis=2, tiled=True
    )
    return (attended.reshape(tokens, width), qkv_grad, filter_grad)


def solution(mesh):
    return jax.shard_map(
        shards,
        mesh=mesh,
        in_specs=(P(("ctx", "tp"), None, None), P(None, None, "tp"), P(), P("ctx", "tp")),
        out_specs=(P("ctx", "tp"), P(("ctx", "tp"), None, None), P(None, None, "tp")),
        check_vma=False,
    )
```

profile of v0, /device:TPU:0, one launch (start us, length us, event | category | flops | bytes accessed | tf_op | source)
XLA Modules:
  0.0 541.6 jit_solution(776772498163065581)
XLA Ops:
  7.2 10.7 %copy.57 = bf16[32,3,8192]{0,1,2:T(4,128)(2,1)} copy(bf16[32,3,8192]{2,0,1:T(8,128)(2,1)} %param.4) | data formatting | bytes 3145728 | tf_op args[0]
  17.8 8.4 %reshape.158 = bf16[4,2,98304]{2,1,0:T(2,128)(2,1)} reshape(bf16[8192,3,32]{2,1,0:T(4,128)(2,1)} %bitcast.114) | data formatting | bytes 3145728
  26.2 4.3 all-to-all-start
  30.7 19.9 %all-to-all-done = bf16[4,2,98304]{2,1,0:T(2,128)(2,1)S(1)} async-done(((bf16[4,2,98304]{2,1,0:T(2,128)(2,1)}), bf16[4,2,98304]{2,1,0:T(2,128)(2,1)S(1)}, u32[]{:S(2)}, u32[]{:S(2)}) %all-to-all-start) | async-done | bytes 1572896 | tf_op jit(solution)/shard_map/all_to_all | solution.py:25
  50.6 7.1 %reshape.159 = bf16[8192,3,32]{2,1,0:T(4,128)(2,1)} reshape(bf16[4,2,98304]{2,1,0:T(2,128)(2,1)S(1)} %all-to-all-done) | data formatting | bytes 3145728
  57.7 10.5 %copy.59 = bf16[4,32,3,2048]{3,1,0,2:T(8,128)(2,1)S(1)} copy(bf16[4,32,3,2048]{1,2,3,0:T(4,128)(2,1)} %bitcast.113) | data formatting | bytes 3145728 | tf_op jit(solution)/shard_map/all_to_all | solution.py:25
  68.2 4.2 collective-permute-start
  72.5 2.1 collective-permute-done
  74.7 1.9 maximum_convert_fusion
  76.6 2.6 add_convert_fusion
  81.5 5.3 collective-permute-start.1
  86.8 20.0 %collective-permute-done.1 = bf16[128,2,2048]{2,0,1:T(8,128)(2,1)} collective-permute-done((bf16[128,2,2048]{2,0,1:T(8,128)(2,1)S(1)}, bf16[128,2,2048]{2,0,1:T(8,128)(2,1)}, u32[]{:S(2)}, u32[]{:S(2)}) %collective-permute-start.1) | collective-permute-done | bytes 1048608 | tf_op jit(solution)/shard_map/ppermute | solution.py:15
  106.8 5.5 %collective-permute-start.2 = (bf16[128,2,2048]{2,0,1:T(8,128)(2,1)}, bf16[128,2,2048]{2,0,1:T(8,128)(2,1)}, u32[]{:S(2)}, u32[]{:S(2)}) collective-permute-start(bf16[128,2,2048]{2,0,1:T(8,128)(2,1)} %collective-permute-done.1), channel_id=1, source_target_pairs={{0,4},{4,8},{8,12},{12,16},{16,20},{20,24},{24,28},{1,5},{5,9},{9,... | collective-permute-start | bytes 3145736 | tf_op jit(solution)/shard_map/ppermute | solution.py:15
  112.8 19.0 %collective-permute-done.2 = bf16[128,2,2048]{2,0,1:T(8,128)(2,1)} collective-permute-done((bf16[128,2,2048]{2,0,1:T(8,128)(2,1)}, bf16[128,2,2048]{2,0,1:T(8,128)(2,1)}, u32[]{:S(2)}, u32[]{:S(2)}) %collective-permute-start.2) | collective-permute-done | bytes 1048608 | tf_op jit(solution)/shard_map/ppermute | solution.py:15
  131.8 6.2 %collective-permute-start.3 = (bf16[128,2,2048]{2,0,1:T(8,128)(2,1)}, bf16[128,2,2048]{2,0,1:T(8,128)(2,1)}, u32[]{:S(2)}, u32[]{:S(2)}) collective-permute-start(bf16[128,2,2048]{2,0,1:T(8,128)(2,1)} %collective-permute-done.2), channel_id=1, source_target_pairs={{0,4},{4,8},{8,12},{12,16},{16,20},{20,24},{24,28},{1,5},{5,9},{9,... | collective-permute-start | bytes 3145736 | tf_op jit(solution)/shard_map/ppermute | solution.py:15
  141.8 14.7 %collective-permute-done.3 = bf16[128,2,2048]{2,0,1:T(8,128)(2,1)} collective-permute-done((bf16[128,2,2048]{2,0,1:T(8,128)(2,1)}, bf16[128,2,2048]{2,0,1:T(8,128)(2,1)}, u32[]{:S(2)}, u32[]{:S(2)}) %collective-permute-start.3) | collective-permute-done | bytes 1048608 | tf_op jit(solution)/shard_map/ppermute | solution.py:15
  156.5 6.3 %collective-permute-start.4 = (bf16[128,2,2048]{2,0,1:T(8,128)(2,1)}, bf16[128,2,2048]{2,0,1:T(8,128)(2,1)}, u32[]{:S(2)}, u32[]{:S(2)}) collective-permute-start(bf16[128,2,2048]{2,0,1:T(8,128)(2,1)} %collective-permute-done.3), channel_id=1, source_target_pairs={{0,4},{4,8},{8,12},{12,16},{16,20},{20,24},{24,28},{1,5},{5,9},{9,... | collective-permute-start | bytes 3145736 | tf_op jit(solution)/shard_map/ppermute | solution.py:15
  163.5 2.0 copy.65
  168.8 2.0 copy.61
  170.8 2.3 constant_dynamic-update-slice_fusion.3
  173.1 2.3 constant_dynamic-update-slice_fusion.2
  175.4 2.3 constant_dynamic-update-slice_fusion.1
  177.8 2.6 collective-permute-done.4
  180.4 2.3 constant_dynamic-update-slice_fusion
  182.7 5.7 %fusion.48 = (bf16[640,1,2048]{2,0,1:T(8,128)(2,1)}, bf16[640,1,2048]{2,0,1:T(8,128)(2,1)}) fusion(bf16[640,2,2048]{2,0,1:T(8,128)(2,1)} %constant_dynamic-update-slice_fusion), kind=kLoop, calls=%fused_computation.106 | loop fusion | bytes 10485760 | tf_op jit(solution)/shard_map/slice | solution.py:47
  188.4 4.4 copy.62
  192.8 4.5 copy.60
  197.2 6.6 %fusion.52 = (f32[16,128]{1,0:T(8,128)S(1)}, f32[16,128,640]{2,1,0:T(8,128)}) fusion(pred[128,640]{1,0:T(8,128)(4,1)} %and_and_fusion, bf16[128,16,128]{0,2,1:T(8,128)(2,1)} %bitcast.124, bf16[640,16,128]{0,2,1:T(8,128)(2,1)} %bitcast.115), kind=kOutput, calls=%fused_computation.110 | convolution fusion | flops 342098560 | bytes 8478720 | tf_op jit(solution)/shard_map/sub | solution.py:71
  203.8 4.1 fusion.18
  210.7 2.6 fusion.2
  213.3 5.3 copy.72
  218.6 6.8 %stack_reshape.7 = f32[5,128,1,2048]{3,1,0,2:T(8,128)} reshape(f32[640,16,128]{2,1,0:T(8,128)} %copy.72) | data formatting | bytes 10485760 | tf_op jit(solution)/shard_map/stack;reshape | solution.py:95
  225.4 5.0 convolution_bitcast_fusion
  230.5 7.4 %reshape.152 = f32[5,128,1,2048]{1,0,3,2:T(8,128)} reshape(f32[640,16,128]{0,2,1:T(8,128)} %convolution_bitcast_fusion) | data formatting | bytes 10485760 | tf_op jit(solution)/shard_map/stack;reshape | solution.py:95
  237.8 7.9 %copy.73 = f32[5,128,1,2048]{3,1,2,0:T(8,128)} copy(f32[5,128,1,2048]{1,0,3,2:T(8,128)} %reshape.152) | data formatting | bytes 10485760 | tf_op jit(solution)/shard_map/stack;reshape | solution.py:95
  249.1 44.7 %collective-permute-done.5 = f32[128,2,2048]{2,0,1:T(8,128)S(1)} collective-permute-done((f32[128,2,2048]{2,0,1:T(8,128)S(1)}, f32[128,2,2048]{2,0,1:T(8,128)S(1)}, u32[]{:S(2)}, u32[]{:S(2)}) %collective-permute-start.5) | collective-permute-done | bytes 2097184 | tf_op jit(solution)/shard_map/ppermute | solution.py:15
  295.7 44.1 %collective-permute-done.6 = f32[128,2,2048]{2,0,1:T(8,128)S(1)} collective-permute-done((f32[128,2,2048]{2,0,1:T(8,128)S(1)}, f32[128,2,2048]{2,0,1:T(8,128)S(1)}, u32[]{:S(2)}, u32[]{:S(2)}) %collective-permute-start.6) | collective-permute-done | bytes 2097184 | tf_op jit(solution)/shard_map/ppermute | solution.py:15
  341.7 42.9 %collective-permute-done.7 = f32[128,2,2048]{2,0,1:T(8,128)S(1)} collective-permute-done((f32[128,2,2048]{2,0,1:T(8,128)S(1)}, f32[128,2,2048]{2,0,1:T(8,128)S(1)}, u32[]{:S(2)}, u32[]{:S(2)}) %collective-permute-start.7) | collective-permute-done | bytes 2097184 | tf_op jit(solution)/shard_map/ppermute | solution.py:15
  387.4 2.1 fusion.53
  389.5 2.5 copy.75
  392.0 37.3 %collective-permute-done.8 = f32[128,2,2048]{2,0,1:T(8,128)} collective-permute-done((f32[128,2,2048]{2,0,1:T(8,128)}, f32[128,2,2048]{2,0,1:T(8,128)}, u32[]{:S(2)}, u32[]{:S(2)}) %collective-permute-start.8) | collective-permute-done | bytes 2097184 | tf_op jit(solution)/shard_map/ppermute | solution.py:15
  429.4 2.5 fusion.33
  431.9 3.6 multiply_reduce_fusion
  437.5 6.2 %collective-permute-done.9 = f32[6,3,2048]{2,0,1:T(8,128)S(1)} collective-permute-done((f32[6,3,2048]{2,0,1:T(8,128)S(1)}, f32[6,3,2048]{2,0,1:T(8,128)S(1)}, u32[]{:S(2)}, u32[]{:S(2)}) %collective-permute-start.9) | collective-permute-done | bytes 147488 | tf_op jit(solution)/shard_map/ppermute | solution.py:15
  444.2 2.6 fusion.5
  446.9 2.7 copy.76
  449.5 3.7 all-to-all-start.1
  456.3 74.4 %all-reduce.2.cloned.1.call-done = f32[3,7,2048]{2,0,1:T(4,128)} async-done(((f32[3,7,2048]{2,0,1:T(4,128)}), f32[3,7,2048]{2,0,1:T(4,128)}) %all-reduce.2.cloned.1.call-update) | async-done | bytes 172048 | tf_op jit(solution)/shard_map/psum | solution.py:114
  (91 shorter events, 32.8 us)
Async XLA Ops:
  26.2 4.3 copy-start.13
  26.2 24.4 %all-to-all-start = ((bf16[4,2,98304]{2,1,0:T(2,128)(2,1)}), bf16[4,2,98304]{2,1,0:T(2,128)(2,1)S(1)}, u32[]{:S(2)}, u32[]{:S(2)}) async-start(bf16[4,2,98304]{2,1,0:T(2,128)(2,1)} %reshape.158), calls=%async_computation | async-start | bytes 3145728 | tf_op jit(solution)/shard_map/all_to_all | solution.py:25
  68.2 4.3 copy-start.5
  68.2 6.4 %collective-permute-start = (bf16[6,3,2048]{2,0,1:T(8,128)(2,1)S(1)}, bf16[6,3,2048]{2,0,1:T(8,128)(2,1)S(1)}, u32[]{:S(2)}, u32[]{:S(2)}) collective-permute-start(bf16[6,3,2048]{2,0,1:T(8,128)(2,1)S(1)} %slice.138), channel_id=1, source_target_pairs={{0,4},{4,8},{8,12},{12,16},{16,20},{20,24},{24,28},{1,5},{5,9},{9,... | collective-permute-start | bytes 221192 | tf_op jit(solution)/shard_map/ppermute | solution.py:15
  72.5 6.7 %copy-start.11 = (f32[3,1,2048]{2,0,1:T(4,128)}, f32[3,1,2048]{2,0,1:T(4,128)S(1)}, u32[]{:S(2)}) copy-start(f32[3,1,2048]{2,0,1:T(4,128)S(1)} %copy.107) | copy-start | bytes 73732
  79.2 1.1 copy-start.6
  80.4 57.7 %copy-start.17 = (s32[8]{0:T(128)S(1)}, s32[8]{0:T(128)}, u32[]{:S(2)}) copy-start(s32[8]{0:T(128)} %param.6) | copy-start | bytes 100
  81.5 25.4 %collective-permute-start.1 = (bf16[128,2,2048]{2,0,1:T(8,128)(2,1)S(1)}, bf16[128,2,2048]{2,0,1:T(8,128)(2,1)}, u32[]{:S(2)}, u32[]{:S(2)}) collective-permute-start(bf16[128,2,2048]{2,0,1:T(8,128)(2,1)S(1)} %get-tuple-element.24), channel_id=1, source_target_pairs={{0,4},{4,8},{8,12},{12,16},{16,20},{20,24},{24,28},{1,5},{5,9},{9,... | collective-permute-start | bytes 3145736 | tf_op jit(solution)/shard_map/ppermute | solution.py:15
  106.8 24.9 %collective-permute-start.2 = (bf16[128,2,2048]{2,0,1:T(8,128)(2,1)}, bf16[128,2,2048]{2,0,1:T(8,128)(2,1)}, u32[]{:S(2)}, u32[]{:S(2)}) collective-permute-start(bf16[128,2,2048]{2,0,1:T(8,128)(2,1)} %collective-permute-done.1), channel_id=1, source_target_pairs={{0,4},{4,8},{8,12},{12,16},{16,20},{20,24},{24,28},{1,5},{5,9},{9,... | collective-permute-start | bytes 3145736 | tf_op jit(solution)/shard_map/ppermute | solution.py:15
  131.8 24.7 %collective-permute-start.3 = (bf16[128,2,2048]{2,0,1:T(8,128)(2,1)}, bf16[128,2,2048]{2,0,1:T(8,128)(2,1)}, u32[]{:S(2)}, u32[]{:S(2)}) collective-permute-start(bf16[128,2,2048]{2,0,1:T(8,128)(2,1)} %collective-permute-done.2), channel_id=1, source_target_pairs={{0,4},{4,8},{8,12},{12,16},{16,20},{20,24},{24,28},{1,5},{5,9},{9,... | collective-permute-start | bytes 3145736 | tf_op jit(solution)/shard_map/ppermute | solution.py:15
  156.5 23.9 %collective-permute-start.4 = (bf16[128,2,2048]{2,0,1:T(8,128)(2,1)}, bf16[128,2,2048]{2,0,1:T(8,128)(2,1)}, u32[]{:S(2)}, u32[]{:S(2)}) collective-permute-start(bf16[128,2,2048]{2,0,1:T(8,128)(2,1)} %collective-permute-done.3), channel_id=1, source_target_pairs={{0,4},{4,8},{8,12},{12,16},{16,20},{20,24},{24,28},{1,5},{5,9},{9,... | collective-permute-start | bytes 3145736 | tf_op jit(solution)/shard_map/ppermute | solution.py:15
  203.8 4.1 copy-start.4
  203.8 5.0 copy-start.7
  203.8 5.0 copy-start.9
  245.7 48.1 %slice-start = ((s8[5242880]{0:T(1024)(128)(4,1)}), s8[4194304]{0:T(1024)(128)(4,1)S(1)}, s32[]{:S(2)}) async-start(s8[5242880]{0:T(1024)(128)(4,1)} %bitcast.108), calls=%async_computation.3 | async-start | bytes 8388608
  245.7 48.1 %slice-start.1 = ((s8[5242880]{0:T(1024)(128)(4,1)}), s8[1048576]{0:T(1024)(128)(4,1)S(1)}, s32[]{:S(2)}) async-start(s8[5242880]{0:T(1024)(128)(4,1)} %bitcast.108), calls=%async_computation.4 | async-start | bytes 2097152
  245.7 48.1 %copy-start = (f32[5,128,1,2048]{3,1,2,0:T(8,128)S(1)}, f32[5,128,1,2048]{3,1,2,0:T(8,128)}, u32[]{:S(2)}) copy-start(f32[5,128,1,2048]{3,1,2,0:T(8,128)} %copy.73) | copy-start | bytes 15728644
  247.5 46.3 %collective-permute-start.5 = (f32[128,2,2048]{2,0,1:T(8,128)S(1)}, f32[128,2,2048]{2,0,1:T(8,128)S(1)}, u32[]{:S(2)}, u32[]{:S(2)}) collective-permute-start(f32[128,2,2048]{2,0,1:T(8,128)S(1)} %fusion.25), channel_id=1, source_target_pairs={{4,0},{8,4},{12,8},{16,12},{20,16},{24,20},{28,24},{5,1},{9,5},{13... | collective-permute-start | bytes 6291464 | tf_op jit(solution)/shard_map/ppermute | solution.py:15
  294.2 45.6 %collective-permute-start.6 = (f32[128,2,2048]{2,0,1:T(8,128)S(1)}, f32[128,2,2048]{2,0,1:T(8,128)S(1)}, u32[]{:S(2)}, u32[]{:S(2)}) collective-permute-start(f32[128,2,2048]{2,0,1:T(8,128)S(1)} %fusion.28), channel_id=1, source_target_pairs={{4,0},{8,4},{12,8},{16,12},{20,16},{24,20},{28,24},{5,1},{9,5},{13... | collective-permute-start | bytes 6291464 | tf_op jit(solution)/shard_map/ppermute | solution.py:15
  340.1 47.3 %copy-start.2 = (bf16[640,1,2048]{0,2,1:T(8,128)(2,1)S(1)}, bf16[640,1,2048]{0,2,1:T(8,128)(2,1)}, u32[]{:S(2)}) copy-start(bf16[640,1,2048]{0,2,1:T(8,128)(2,1)} %copy.62) | copy-start | bytes 7864324
  340.1 47.3 %copy-start.3 = (bf16[16,128,640]{2,1,0:T(8,128)(2,1)S(1)}, bf16[16,128,640]{2,1,0:T(8,128)(2,1)}, u32[]{:S(2)}) copy-start(bf16[16,128,640]{2,1,0:T(8,128)(2,1)} %fusion.2) | copy-start | bytes 7864324
  340.1 44.4 %collective-permute-start.7 = (f32[128,2,2048]{2,0,1:T(8,128)S(1)}, f32[128,2,2048]{2,0,1:T(8,128)S(1)}, u32[]{:S(2)}, u32[]{:S(2)}) collective-permute-start(f32[128,2,2048]{2,0,1:T(8,128)S(1)} %fusion.31), channel_id=1, source_target_pairs={{4,0},{8,4},{12,8},{16,12},{20,16},{24,20},{28,24},{5,1},{9,5},{13... | collective-permute-start | bytes 6291464 | tf_op jit(solution)/shard_map/ppermute | solution.py:15
  386.1 43.2 %collective-permute-start.8 = (f32[128,2,2048]{2,0,1:T(8,128)}, f32[128,2,2048]{2,0,1:T(8,128)}, u32[]{:S(2)}, u32[]{:S(2)}) collective-permute-start(f32[128,2,2048]{2,0,1:T(8,128)} %fusion.23), channel_id=1, source_target_pairs={{4,0},{8,4},{12,8},{16,12},{20,16},{24,20},{28,24},{5,1},{9,5},{13... | collective-permute-start | bytes 6291464 | tf_op jit(solution)/shard_map/ppermute | solution.py:15
  392.0 39.8 %copy-start.1 = (f32[128,1,2048]{2,0,1:T(8,128)S(1)}, f32[128,1,2048]{2,0,1:T(8,128)}, u32[]{:S(2)}) copy-start(f32[128,1,2048]{2,0,1:T(8,128)} %copy.75) | copy-start | bytes 3145732
  435.5 8.3 %collective-permute-start.9 = (f32[6,3,2048]{2,0,1:T(8,128)S(1)}, f32[6,3,2048]{2,0,1:T(8,128)S(1)}, u32[]{:S(2)}, u32[]{:S(2)}) collective-permute-start(f32[6,3,2048]{2,0,1:T(8,128)S(1)} %fusion.45), channel_id=1, source_target_pairs={{4,0},{8,4},{12,8},{16,12},{20,16},{24,20},{28,24},{5,1},{9,5},{13... | collective-permute-start | bytes 442376 | tf_op jit(solution)/shard_map/ppermute | solution.py:15
  436.8 0.7 copy-start.10
  437.5 6.6 %copy-start.12 = (f32[3,1,2048]{2,0,1:T(4,128)S(1)}, f32[3,1,2048]{2,0,1:T(4,128)}, u32[]{:S(2)}) copy-start(f32[3,1,2048]{2,0,1:T(4,128)} %copy-done.11) | copy-start | bytes 73732
  446.8 6.5 %copy-start.16 = (f32[3,2048]{1,0:T(4,128)S(1)}, f32[3,2048]{1,0:T(4,128)}, u32[]{:S(2)}) copy-start(f32[3,2048]{1,0:T(4,128)} %get-tuple-element.17) | copy-start | bytes 73732
  446.8 7.2 %copy-start.15 = (f32[3,2048]{1,0:T(4,128)S(1)}, f32[3,2048]{1,0:T(4,128)}, u32[]{:S(2)}) copy-start(f32[3,2048]{1,0:T(4,128)} %get-tuple-element.16) | copy-start | bytes 73732
  446.8 7.8 %copy-start.14 = (f32[3,2048]{1,0:T(4,128)S(1)}, f32[3,2048]{1,0:T(4,128)}, u32[]{:S(2)}) copy-start(f32[3,2048]{1,0:T(4,128)} %get-tuple-element.15) | copy-start | bytes 73732
  449.5 5.7 %copy-start.8 = (bf16[128,16,128]{0,2,1:T(8,128)(2,1)S(1)}, bf16[128,16,128]{0,2,1:T(8,128)(2,1)}, u32[]{:S(2)}) copy-start(bf16[128,16,128]{0,2,1:T(8,128)(2,1)} %get-tuple-element.41) | copy-start | bytes 1572868
  449.5 82.8 %all-to-all-start.1 = ((bf16[128,3,2048]{2,1,0:T(4,128)(2,1)}), bf16[128,3,2048]{2,1,0:T(4,128)(2,1)S(1)}, u32[]{:S(2)}, u32[]{:S(2)}) async-start(bf16[128,3,2048]{2,1,0:T(4,128)(2,1)} %copy.76), calls=%async_computation.1 | async-start | bytes 4194304 | tf_op jit(solution)/shard_map/all_to_all | solution.py:115
  453.3 77.4 %all-reduce.2.cloned.1.call-start = ((), (), s32[]{:S(2)}) async-start(), calls=%async_computation.2 | async-start | bytes 458752 | tf_op jit(solution)/shard_map/psum | solution.py:114
Sparse Core Ops, SparseCore 0:
  458.1 72.5 all-reduce.1
where the time goes:
time: 544 us; the launch traced here: 542 us
  waiting for transfers between devices  328 us (60%)
  local copies, waits for them, and re-layouts  114 us (21%)
  starting transfers between devices  42.9 us (8%)
  matrix products  22.2 us (4%)
  other arithmetic  20.2 us (4%)
  between operations  14.5 us (3%)
    ppermute x10, waiting for transfers between devices, from_behind(): lax.ppermute(value, axis, [(source, source + steps) for source in range(f...  234 us
    psum x1, waiting for transfers between devices, shards(): filter_grad = lax.psum(tap_terms, 'ctx')  74.4 us
    unnamed x63, local copies, waits for them, and re-layouts  44.5 us
    ppermute x10, starting transfers between devices, from_behind(): lax.ppermute(value, axis, [(source, source + steps) for source in range(f...  34.8 us
    another operation x3, local copies, waits for them, and re-layouts, shards(): jnp.stack([key_part.reshape(reach, tokens, width), value_part.reshape(rea...  22 us
    all_to_all x1, waiting for transfers between devices, shards(): local = lax.all_to_all(qkv, 'tp', split_axis=2, concat_axis=0, tiled=True)  19.9 us
  transfers between devices with their start and end apart: 13, of which 12 were waited for; matrix products, arithmetic and copies ran while one was open for 5% of the time, Pallas kernels for 0%

commit v1 on v0

--- a/solution.py
+++ b/solution.py
@@ -1,12 +1,292 @@
 import jax
 import jax.numpy as jnp
 from jax import lax
+from jax.experimental import pallas as pl
+from jax.experimental.pallas import tpu as pltpu
 from jax.sharding import PartitionSpec as P
 
 HEAD_DIM = 128
 KW = 7
 BLOCK = 128
 STEPS = 4
+PAD = 8
+SCALE = HEAD_DIM ** (-0.5)
+AXES = ("ctx", "tp")
+
+
+def dot(a, b, dims):
+    return lax.dot_general(a, b, (dims, ((), ())), preferred_element_type=jnp.float32)
+
+
+def estimate(flops, moved):
+    return pl.CostEstimate(flops=flops, bytes_accessed=moved, transcendentals=0)
+
+
+def pack_qkv(x, members):
+    streams, rows, channels = x.shape
+    tp = lax.axis_size("tp")
+    width = channels // tp
+    per = width // HEAD_DIM // members
+
+    def kernel(x_ref, o_ref):
+        for c in range(members):
+            for j in range(per):
+                at = (c * per + j) * HEAD_DIM
+                o_ref[c, 0, j] = x_ref[:, :, at : at + HEAD_DIM]
+
+    return pl.pallas_call(
+        kernel,
+        grid=(tp,),
+        in_specs=[pl.BlockSpec((streams, rows, width), lambda t: (0, 0, t))],
+        out_specs=pl.BlockSpec(
+            (members, 1, per, streams, rows, HEAD_DIM), lambda t: (0, t, 0, 0, 0, 0)
+        ),
+        out_shape=jax.ShapeDtypeStruct((members, tp, per, streams, rows, HEAD_DIM), x.dtype),
+        cost_estimate=estimate(0, 4 * x.size),
+        name="pack_qkv",
+    )(x)
+
+
+def unpack_qkv(x, members):
+    _, tp, per, streams, rows, _ = x.shape
+    width = members * per * HEAD_DIM
+
+    def kernel(x_ref, o_ref):
+        for c in range(members):
+            for j in range(per):
+                at = (c * per + j) * HEAD_DIM
+                o_ref[:, :, at : at + HEAD_DIM] = x_ref[c, 0, j]
+
+    return pl.pallas_call(
+        kernel,
+        grid=(tp,),
+        in_specs=[
+            pl.BlockSpec((members, 1, per, streams, rows, HEAD_DIM), lambda t: (0, t, 0, 0, 0, 0))
+        ],
+        out_specs=pl.BlockSpec((streams, rows, width), lambda t: (0, 0, t)),
+        out_shape=jax.ShapeDtypeStruct((streams, rows, tp * width), x.dtype),
+        cost_estimate=estimate(0, 4 * x.size),
+        name="unpack_qkv",
+    )(x)
+
+
+def pack_rows(x, members):
+    tokens, width = x.shape
+    per = width // HEAD_DIM // members
+
+    def kernel(x_ref, o_ref):
+        for c in range(members):
+            for j in range(per):
+                at = (c * per + j) * HEAD_DIM
+                o_ref[c, j] = x_ref[:, at : at + HEAD_DIM]
+
+    return pl.pallas_call(
+        kernel,
+        out_shape=jax.ShapeDtypeStruct((members, per, tokens, HEAD_DIM), x.dtype),
+        cost_estimate=estimate(0, 4 * x.size),
+        name="pack_rows",
+    )(x)
+
+
+def unpack_rows(x):
+    members, per, tokens, _ = x.shape
+
+    def kernel(x_ref, o_ref):
+        for c in range(members):
+            for j in range(per):
+                at = (c * per + j) * HEAD_DIM
+                o_ref[:, at : at + HEAD_DIM] = x_ref[c, j]
+
+    return pl.pallas_call(
+        kernel,
+        out_shape=jax.ShapeDtypeStruct((tokens, members * per * HEAD_DIM), x.dtype),
+        cost_estimate=estimate(0, 4 * x.size),
+        name="unpack_rows",
+    )(x)
+
+
+def masked_scores(docs, query, keys, block, first):
+    raw = dot(query, keys, ((1,), (1,))) * SCALE
+    rows = lax.broadcasted_iota(jnp.int32, (BLOCK, BLOCK), 0)
+    cols = lax.broadcasted_iota(jnp.int32, (BLOCK, BLOCK), 1)
+    tiles = []
+    for other in range(first, block + 1):
+        tile = raw[:, (other - first) * BLOCK : (other - first + 1) * BLOCK]
+        if other == block:
+            tile = jnp.where(cols <= rows, tile, -1e30)
+        else:
+            tile = jnp.where(docs[other] == docs[block], tile, -1e30)
+        tiles.append(tile)
+    masked = jnp.concatenate(tiles, axis=1) if len(tiles) > 1 else tiles[0]
+    row_max = jnp.max(masked, axis=1, keepdims=True)
+    expo = jnp.exp(masked - row_max)
+    return expo, jnp.sum(expo, axis=1, keepdims=True)
+
+
+def forward_kernel(docs, x_ref, taps_ref, mixed_ref, out_ref, padded):
+    sources, _, streams, rows, _ = x_ref.shape
+    tokens = sources * rows
+    padded[:, 0:PAD, :] = jnp.zeros((streams, PAD, HEAD_DIM), jnp.float32)
+    for m in range(streams):
+        padded[m, PAD:, :] = x_ref[:, 0, m].reshape(tokens, HEAD_DIM).astype(jnp.float32)
+    for m in range(streams):
+        for start in range(0, tokens, BLOCK):
+            total = jnp.zeros((BLOCK, HEAD_DIM), jnp.float32)
+            for lag in range(KW):
+                at = PAD + start - lag
+                total = total + taps_ref[m, lag : lag + 1, :] * padded[m, at : at + BLOCK, :]
+            mixed_ref[0, m, start : start + BLOCK, :] = total.astype(jnp.bfloat16)
+    for block in range(tokens // BLOCK):
+        first = max(0, block - STEPS)
+        own = slice(block * BLOCK, (block + 1) * BLOCK)
+        span = slice(first * BLOCK, (block + 1) * BLOCK)
+        expo, row_sum = masked_scores(
+            docs, mixed_ref[0, 0, own, :], mixed_ref[0, 1, span, :], block, first
+        )
+        total = dot(expo.astype(jnp.bfloat16), mixed_ref[0, 2, span, :], ((1,), (0,)))
+        per = out_ref.shape[2]
+        at = block * BLOCK
+        out_ref[at // per, 0, at % per : at % per + BLOCK, :] = (total / row_sum).astype(
+            jnp.bfloat16
+        )
+
+
+def forward(docs, x, taps, members):
+    sources, per, streams, rows, _ = x.shape
+    tokens = sources * rows
+    return pl.pallas_call(
+        forward_kernel,
+        grid_spec=pltpu.PrefetchScalarGridSpec(
+            num_scalar_prefetch=1,
+            grid=(per,),
+            in_specs=[
+                pl.BlockSpec((sources, 1, streams, rows, HEAD_DIM), lambda h, d: (0, h, 0, 0, 0)),
+                pl.BlockSpec((streams, KW, HEAD_DIM), lambda h, d: (0, 0, h)),
+            ],
+            out_specs=[
+                pl.BlockSpec((1, streams, tokens, HEAD_DIM), lambda h, d: (h, 0, 0, 0)),
+                pl.BlockSpec((members, 1, tokens // members, HEAD_DIM), lambda h, d: (0, h, 0, 0)),
+            ],
+            scratch_shapes=[pltpu.VMEM((streams, tokens + PAD, HEAD_DIM), jnp.float32)],
+        ),
+        out_shape=[
+            jax.ShapeDtypeStruct((per, streams, tokens, HEAD_DIM), jnp.bfloat16),
+            jax.ShapeDtypeStruct((members, per, tokens // members, HEAD_DIM), jnp.bfloat16),
+        ],
+        cost_estimate=estimate(10_000_000_000, 8 * x.size),
+        name="forward",
+    )(docs, x, taps)
+
+
+def backward_kernel(
+    docs, x_ref, taps_ref, mixed_ref, att_ref, up_ref, grad_ref, tapg_ref, padded, cgrad
+):
+    sources, _, streams, rows, _ = x_ref.shape
+    tokens = sources * rows
+    per = att_ref.shape[2]
+    cgrad[...] = jnp.zeros_like(cgrad)
+    for block in range(tokens // BLOCK):
+        first = max(0, block - STEPS)
+        own = slice(block * BLOCK, (block + 1) * BLOCK)
+        span = slice(first * BLOCK, (block + 1) * BLOCK)
+        query, keys, values = (
+            mixed_ref[0, 0, own, :],
+            mixed_ref[0, 1, span, :],
+            mixed_ref[0, 2, span, :],
+        )
+        at = block * BLOCK
+        up = up_ref[at // per, 0, at % per : at % per + BLOCK, :]
+        att = att_ref[at // per, 0, at % per : at % per + BLOCK, :]
+        delta = jnp.sum(up.astype(jnp.float32) * att.astype(jnp.float32), axis=1, keepdims=True)
+        expo, row_sum = masked_scores(docs, query, keys, block, first)
+        prob = expo / row_sum
+        dprob = dot(up, values, ((1,), (1,)))
+        dscore = (prob * (dprob - delta) * SCALE).astype(jnp.bfloat16)
+        cgrad[0, own, :] = dot(dscore, keys, ((1,), (0,)))
+        cgrad[1, span, :] += dot(dscore, query, ((0,), (0,)))
+        cgrad[2, span, :] += dot(prob.astype(jnp.bfloat16), up, ((0,), (0,)))
+    padded[:, 0:PAD, :] = jnp.zeros((streams, PAD, HEAD_DIM), jnp.float32)
+    for m in range(streams):
+        padded[m, PAD:, :] = x_ref[:, 0, m].reshape(tokens, HEAD_DIM).astype(jnp.float32)
+    for m in range(streams):
+        sums = [jnp.zeros((8, HEAD_DIM), jnp.float32) for _ in range(KW)]
+        for start in range(0, tokens, BLOCK):
+            total = jnp.zeros((BLOCK, HEAD_DIM), jnp.float32)
+            here = cgrad[m, start : start + BLOCK, :]
+            for lag in range(KW):
+                total = (
+                    total
+                    + taps_ref[m, lag : lag + 1, :]
+                    * cgrad[m, start + lag : start + lag + BLOCK, :]
+                )
+                at = PAD + start - lag
+                product = padded[m, at : at + BLOCK, :] * here
+                sums[lag] = sums[lag] + jnp.sum(product.reshape(BLOCK // 8, 8, HEAD_DIM), axis=0)
+            grad_ref[start // rows : (start + BLOCK) // rows, 0, m] = total.astype(
+                jnp.bfloat16
+            ).reshape(BLOCK // rows, rows, HEAD_DIM)
+        for lag in range(KW):
+            tapg_ref[m, lag : lag + 1, :] = jnp.sum(sums[lag], axis=0, keepdims=True)
+
+
+def backward(docs, x, taps, mixed, att, up):
+    sources, per, streams, rows, _ = x.shape
+    tokens = sources * rows
+    members = att.shape[0]
+    slab = pl.BlockSpec((sources, 1, streams, rows, HEAD_DIM), lambda h, d: (0, h, 0, 0, 0))
+    tap = pl.BlockSpec((streams, KW, HEAD_DIM), lambda h, d: (0, 0, h))
+    rowspec = pl.BlockSpec((members, 1, tokens // members, HEAD_DIM), lambda h, d: (0, h, 0, 0))
+    return pl.pallas_call(
+        backward_kernel,
+        grid_spec=pltpu.PrefetchScalarGridSpec(
+            num_scalar_prefetch=1,
+            grid=(per,),
+            in_specs=[
+                slab,
+                tap,
+                pl.BlockSpec((1, streams, tokens, HEAD_DIM), lambda h, d: (h, 0, 0, 0)),
+                rowspec,
+                rowspec,
+            ],
+            out_specs=[slab, tap],
+            scratch_shapes=[
+                pltpu.VMEM((streams, tokens + PAD, HEAD_DIM), jnp.float32),
+                pltpu.VMEM((streams, tokens + PAD, HEAD_DIM), jnp.float32),
+            ],
+        ),
+        out_shape=[
+            jax.ShapeDtypeStruct(x.shape, jnp.bfloat16),
+            jax.ShapeDtypeStruct(taps.shape, jnp.float32),
+        ],
+        cost_estimate=estimate(20_000_000_000, 12 * x.size),
+        name="backward",
+    )(docs, x, taps, mixed, att, up)
+
+
+def swap(value, axes):
+    shape = value.shape
+    return lax.all_to_all(
+        value.reshape(shape[0], -1, HEAD_DIM), axes, split_axis=0, concat_axis=0, tiled=True
+    ).reshape(shape)
+
+
+def by_heads(qkv, filters, doc_ids, upstream):
+    members, tp = lax.axis_size("ctx"), lax.axis_size("tp")
+    rows, streams, _ = qkv.shape
+    per = upstream.shape[1] // HEAD_DIM // members
+    position = lax.axis_index("ctx")
+    packed = pack_qkv(jnp.transpose(qkv, (1, 0, 2)), members)
+    x = swap(packed.reshape((members * tp,) + packed.shape[2:]), AXES)
+    up = swap(pack_rows(upstream, members), "ctx")
+    taps = lax.dynamic_slice_in_dim(filters, position * per * HEAD_DIM, per * HEAD_DIM, 2)
+    mixed, att = forward(doc_ids, x, taps, members)
+    attended = unpack_rows(swap(att, "ctx"))
+    grad, tap_grad = backward(doc_ids, x, taps, mixed, att, up)
+    grad = swap(grad, AXES)
+    qkv_grad = unpack_qkv(grad.reshape((members, tp) + grad.shape[1:]), members)
+    pieces = lax.all_gather(tap_grad, "ctx", axis=0)
+    filter_grad = jnp.transpose(pieces, (1, 2, 0, 3)).reshape(filters.shape)
+    return attended, jnp.transpose(qkv_grad, (1, 0, 2)), filter_grad
 
 
 def from_behind(value, axis, steps):
@@ -21,7 +301,7 @@
     return jnp.repeat(picked, BLOCK)
 
 
-def shards(qkv, filters, doc_ids, upstream):
+def by_ring(qkv, filters, doc_ids, upstream):
     local = lax.all_to_all(qkv, "tp", split_axis=2, concat_axis=0, tiled=True)
     tokens = local.shape[0]
     width = local.shape[2]
@@ -119,6 +399,13 @@
 
 
 def solution(mesh):
+    def shards(qkv, filters, doc_ids, upstream):
+        heads = upstream.shape[1] // HEAD_DIM
+        tokens = upstream.shape[0]
+        whole = heads % mesh.shape["ctx"] == 0 and tokens % BLOCK == 0
+        form = by_heads if whole else by_ring
+        return form(qkv, filters, doc_ids, upstream)
+
     return jax.shard_map(
         shards,
         mesh=mesh,

time: 544 us -> 158 us (0.29)
  waiting for transfers between devices: 328 us -> 43.1 us
  local copies, waits for them, and re-layouts: 114 us -> 3.37 us
  blocking collectives: 0 us -> 57.9 us
  Pallas kernels: 0 us -> 32.7 us
  starting transfers between devices: 42.9 us -> 19.7 us
  matrix products: 22.2 us -> 0 us
  other arithmetic: 20.2 us -> 0 us
  between operations: 14.5 us -> 0.7 us
    ppermute x10 -> x0, waiting for transfers between devices: 234 us -> none  [from_behind(): lax.ppermute(value, axis, [(source, source + steps) for source in range(f...]
    psum x1 -> x0, waiting for transfers between devices: 74.4 us -> none  [shards(): filter_grad = lax.psum(tap_terms, 'ctx')]
    all_gather x0 -> x1, blocking collectives: none -> 57.9 us  [by_heads(): pieces = lax.all_gather(tap_grad, 'ctx', axis=0)]
    unnamed x63 -> x12, local copies, waits for them, and re-layouts: 44.5 us -> 1.98 us
    ppermute x10 -> x0, starting transfers between devices: 34.8 us -> none  [from_behind(): lax.ppermute(value, axis, [(source, source + steps) for source in range(f...]
    pallas_call x0 -> x6, Pallas kernels: none -> 32.7 us  [the longest x1 13.5 us: backward(): pl.pallas_call(backward_kernel, grid_spec=pltpu.PrefetchScalarGridSpec(nu...]
    all_to_all x2 -> x4, waiting for transfers between devices: 19.9 us -> 43.1 us  [swap(): lax.all_to_all(value.reshape(shape[0], -1, HEAD_DIM), axes, split_axis=0,...]
    another operation x4 -> x0, local copies, waits for them, and re-layouts: 22.6 us -> none  [the longest x3 22 us: shards(): jnp.stack([key_part.reshape(reach, tokens, width), value_part.reshape(rea...]
  transfers between devices with their start and end apart: 13 -> 4, of which waited for: 12 -> 3; matrix products, arithmetic and copies ran while one was open for 5% -> 1% of each run, Pallas kernels for 0% -> 16%
where the time goes in v1:
time: 158 us; the launch traced here: 157 us
  blocking collectives  57.9 us (37%)
  waiting for transfers between devices  43.1 us (27%)
  Pallas kernels  32.7 us (21%)
  starting transfers between devices  19.7 us (12%)
  local copies, waits for them, and re-layouts  3.37 us (2%)
    all_gather x1, blocking collectives, by_heads(): pieces = lax.all_gather(tap_grad, 'ctx', axis=0)  57.9 us
    all_to_all x4, waiting for transfers between devices, swap(): lax.all_to_all(value.reshape(shape[0], -1, HEAD_DIM), axes, split_axis=0,...  43.1 us
    all_to_all x4, starting transfers between devices, swap(): lax.all_to_all(value.reshape(shape[0], -1, HEAD_DIM), axes, split_axis=0,...  19.7 us
    pallas_call x1, Pallas kernels, backward(): pl.pallas_call(backward_kernel, grid_spec=pltpu.PrefetchScalarGridSpec(nu...  13.5 us
    pallas_call x1, Pallas kernels, forward(): pl.pallas_call(forward_kernel, grid_spec=pltpu.PrefetchScalarGridSpec(num...  7.82 us
    pallas_call x1, Pallas kernels, unpack_qkv(): pl.pallas_call(kernel, grid=(tp,), in_specs=[pl.BlockSpec((members, 1, pe...  3.7 us
    pallas_call x1, Pallas kernels, pack_qkv(): pl.pallas_call(kernel, grid=(tp,), in_specs=[pl.BlockSpec((streams, rows,...  3.69 us
  transfers between devices with their start and end apart: 4, of which 3 were waited for; matrix products, arithmetic and copies ran while one was open for 1% of the time, Pallas kernels for 16%

profile of v1, /device:TPU:0, one launch (start us, length us, event | category | flops | bytes accessed | tf_op | source)
XLA Modules:
  0.0 157.4 jit_solution(3434189522739713870)
XLA Ops:
  0.6 0.0 copy-start
  0.6 3.7 %pack_qkv.1 = bf16[8,4,2,3,32,128]{5,4,3,2,1,0:T(8,128)(2,1)} custom-call(bf16[3,32,8192]{2,1,0:T(8,128)(2,1)} %bitcast.19), custom_call_target="tpu_custom_call" | custom-call | bytes 3145728 | tf_op jit(solution)/shard_map/pack_qkv/pallas_call | solution.py:37
  4.3 7.3 %all-to-all-start = ((bf16[32,192,128]{2,1,0:T(8,128)(2,1)}), bf16[32,192,128]{2,1,0:T(8,128)(2,1)S(1)}, u32[]{:S(2)}, u32[]{:S(2)}) async-start(bf16[32,192,128]{2,1,0:T(8,128)(2,1)} %bitcast.15), calls=%async_computation | async-start | bytes 3145728 | tf_op jit(solution)/shard_map/all_to_all | solution.py:268
  11.6 1.9 %pack_rows.1 = bf16[8,2,128,128]{3,2,1,0:T(8,128)(2,1)} custom-call(bf16[128,2048]{1,0:T(8,128)(2,1)} %x_ref.1), custom_call_target="tpu_custom_call" | custom-call | bytes 1048576 | tf_op jit(solution)/shard_map/pack_rows/pallas_call | solution.py:83
  13.6 0.0 copy-done
  13.6 0.6 constant_dynamic-slice_fusion.taps_ref
  14.2 35.2 %all-to-all-done = bf16[32,192,128]{2,1,0:T(8,128)(2,1)S(1)} async-done(((bf16[32,192,128]{2,1,0:T(8,128)(2,1)}), bf16[32,192,128]{2,1,0:T(8,128)(2,1)S(1)}, u32[]{:S(2)}, u32[]{:S(2)}) %all-to-all-start) | async-done | bytes 1572896 | tf_op jit(solution)/shard_map/all_to_all | solution.py:268
  49.4 0.0 copy-start.3
  49.4 3.5 %all-to-all-start.2 = ((bf16[8,256,128]{2,1,0:T(8,128)(2,1)}), bf16[8,256,128]{2,1,0:T(8,128)(2,1)S(1)}, u32[]{:S(2)}, u32[]{:S(2)}) async-start(bf16[8,256,128]{2,1,0:T(8,128)(2,1)} %bitcast.18), calls=%async_computation.2 | async-start | bytes 1048576 | tf_op jit(solution)/shard_map/all_to_all | solution.py:268
  52.9 0.0 copy-done.3
  52.9 7.8 %forward.1 = (bf16[2,3,1024,128]{3,2,1,0:T(8,128)(2,1)}, bf16[8,2,128,128]{3,2,1,0:T(8,128)(2,1)}) custom-call(s32[8]{0:T(128)} %docs.3, bf16[32,2,3,32,128]{4,3,2,1,0:T(8,128)(2,1)} %bitcast.20, f32[3,7,256]{2,1,0:T(8,128)} %constant_dynamic-slice_fusion.taps_ref), custom_call_target="tpu_custom_call" | custom-call | flops 10000000000 | bytes 6291456 | tf_op jit(solution)/shard_map/forward/pallas_call | solution.py:157
  60.7 6.8 %all-to-all-done.2 = bf16[8,256,128]{2,1,0:T(8,128)(2,1)S(1)} async-done(((bf16[8,256,128]{2,1,0:T(8,128)(2,1)}), bf16[8,256,128]{2,1,0:T(8,128)(2,1)S(1)}, u32[]{:S(2)}, u32[]{:S(2)}) %all-to-all-start.2) | async-done | bytes 524320 | tf_op jit(solution)/shard_map/all_to_all | solution.py:268
  67.5 0.0 copy-start.4
  67.5 3.6 %all-to-all-start.1 = ((bf16[8,256,128]{2,1,0:T(8,128)(2,1)}), bf16[8,256,128]{2,1,0:T(8,128)(2,1)S(1)}, u32[]{:S(2)}, u32[]{:S(2)}) async-start(bf16[8,256,128]{2,1,0:T(8,128)(2,1)} %bitcast.26), calls=%async_computation.1 | async-start | bytes 1048576 | tf_op jit(solution)/shard_map/all_to_all | solution.py:268
  71.1 0.0 copy-done.4
  71.1 13.5 %backward.1 = (bf16[32,2,3,32,128]{4,3,2,1,0:T(8,128)(2,1)}, f32[3,7,256]{2,1,0:T(8,128)}) custom-call(s32[8]{0:T(128)} %docs.3, bf16[32,2,3,32,128]{4,3,2,1,0:T(8,128)(2,1)} %bitcast.21, f32[3,7,256]{2,1,0:T(8,128)} %constant_dynamic-slice_fusion.taps_ref, bf16[2,3,1024,128]{3,2,1,0:T(8,128)(2,1)} %get-tuple-element.8.mixed_ref, ...), custom_call_target="tpu_custom_call" | custom-call | flops 20000000000 | bytes 9437184 | tf_op jit(solution)/shard_map/backward/pallas_call | solution.py:239
  84.7 1.1 all-to-all-done.1
  85.8 0.0 copy-start.2
  85.8 0.0 copy-start.5
  85.8 0.8 copy-done.2
  86.6 5.3 %all-to-all-start.3 = ((bf16[32,192,128]{2,1,0:T(8,128)(2,1)}), bf16[32,192,128]{2,1,0:T(8,128)(2,1)S(1)}, u32[]{:S(2)}, u32[]{:S(2)}) async-start(bf16[32,192,128]{2,1,0:T(8,128)(2,1)} %bitcast.22), calls=%async_computation.3 | async-start | bytes 3145728 | tf_op jit(solution)/shard_map/all_to_all | solution.py:268
  91.9 0.0 copy-done.5
  91.9 57.9 %all-gather = f32[24,7,256]{2,1,0:T(8,128)S(1)} all-gather(f32[3,7,256]{2,1,0:T(8,128)S(1)} %copy-done.5), channel_id=2, replica_groups=mesh['ctx'=8,'tp'=4] {'ctx'}, dimensions={0}, use_global_device_ids=true | all-gather | bytes 193536 | tf_op jit(solution)/shard_map/all_gather | solution.py:287
  149.7 0.1 copy.8
  149.8 0.7 reshape.33
  150.5 2.0 %unpack_rows.1 = bf16[128,2048]{1,0:T(8,128)(2,1)} custom-call(bf16[8,2,128,128]{3,2,1,0:T(8,128)(2,1)} %bitcast.17), custom_call_target="tpu_custom_call" | custom-call | bytes 1048576 | tf_op jit(solution)/shard_map/unpack_rows/pallas_call | solution.py:100
  152.5 0.0 all-to-all-done.3
  152.5 0.0 copy-start.1
  152.5 1.2 copy-done.1
  153.7 3.7 %unpack_qkv.1 = bf16[3,32,8192]{2,1,0:T(8,128)(2,1)} custom-call(bf16[8,4,2,3,32,128]{5,4,3,2,1,0:T(8,128)(2,1)} %bitcast.16), custom_call_target="tpu_custom_call" | custom-call | bytes 3145728 | tf_op jit(solution)/shard_map/unpack_qkv/pallas_call | solution.py:60
Async XLA Ops:
  0.6 13.0 %copy-start = (f32[3,7,2048]{2,1,0:T(8,128)S(1)}, f32[3,7,2048]{2,1,0:T(8,128)}, u32[]{:S(2)}) copy-start(f32[3,7,2048]{2,1,0:T(8,128)} %param.5) | copy-start | bytes 516100
  4.3 45.0 %all-to-all-start = ((bf16[32,192,128]{2,1,0:T(8,128)(2,1)}), bf16[32,192,128]{2,1,0:T(8,128)(2,1)S(1)}, u32[]{:S(2)}, u32[]{:S(2)}) async-start(bf16[32,192,128]{2,1,0:T(8,128)(2,1)} %bitcast.15), calls=%async_computation | async-start | bytes 3145728 | tf_op jit(solution)/shard_map/all_to_all | solution.py:268
  49.4 3.5 %copy-start.3 = (bf16[32,192,128]{2,1,0:T(8,128)(2,1)}, bf16[32,192,128]{2,1,0:T(8,128)(2,1)S(1)}, u32[]{:S(2)}) copy-start(bf16[32,192,128]{2,1,0:T(8,128)(2,1)S(1)} %all-to-all-done) | copy-start | bytes 4718596
  49.4 18.1 %all-to-all-start.2 = ((bf16[8,256,128]{2,1,0:T(8,128)(2,1)}), bf16[8,256,128]{2,1,0:T(8,128)(2,1)S(1)}, u32[]{:S(2)}, u32[]{:S(2)}) async-start(bf16[8,256,128]{2,1,0:T(8,128)(2,1)} %bitcast.18), calls=%async_computation.2 | async-start | bytes 1048576 | tf_op jit(solution)/shard_map/all_to_all | solution.py:268
  67.5 3.6 %copy-start.4 = (bf16[8,256,128]{2,1,0:T(8,128)(2,1)}, bf16[8,256,128]{2,1,0:T(8,128)(2,1)S(1)}, u32[]{:S(2)}) copy-start(bf16[8,256,128]{2,1,0:T(8,128)(2,1)S(1)} %all-to-all-done.2) | copy-start | bytes 1572868
  67.5 18.3 %all-to-all-start.1 = ((bf16[8,256,128]{2,1,0:T(8,128)(2,1)}), bf16[8,256,128]{2,1,0:T(8,128)(2,1)S(1)}, u32[]{:S(2)}, u32[]{:S(2)}) async-start(bf16[8,256,128]{2,1,0:T(8,128)(2,1)} %bitcast.26), calls=%async_computation.1 | async-start | bytes 1048576 | tf_op jit(solution)/shard_map/all_to_all | solution.py:268
  85.8 0.8 copy-start.2
  85.8 6.1 %copy-start.5 = (f32[3,7,256]{2,1,0:T(8,128)S(1)}, f32[3,7,256]{2,1,0:T(8,128)}, u32[]{:S(2)}) copy-start(f32[3,7,256]{2,1,0:T(8,128)} %get-tuple-element.10) | copy-start | bytes 64516
  86.6 65.9 %all-to-all-start.3 = ((bf16[32,192,128]{2,1,0:T(8,128)(2,1)}), bf16[32,192,128]{2,1,0:T(8,128)(2,1)S(1)}, u32[]{:S(2)}, u32[]{:S(2)}) async-start(bf16[32,192,128]{2,1,0:T(8,128)(2,1)} %bitcast.22), calls=%async_computation.3 | async-start | bytes 3145728 | tf_op jit(solution)/shard_map/all_to_all | solution.py:268
  152.5 1.2 copy-start.1

commit v2 on v1

--- a/solution.py
+++ b/solution.py
@@ -22,86 +22,52 @@
     return pl.CostEstimate(flops=flops, bytes_accessed=moved, transcendentals=0)
 
 
-def pack_qkv(x, members):
-    streams, rows, channels = x.shape
-    tp = lax.axis_size("tp")
-    width = channels // tp
-    per = width // HEAD_DIM // members
-
-    def kernel(x_ref, o_ref):
-        for c in range(members):
-            for j in range(per):
-                at = (c * per + j) * HEAD_DIM
-                o_ref[c, 0, j] = x_ref[:, :, at : at + HEAD_DIM]
+def split_columns(x, members, place):
+    *outer, channels = x.shape
+    width = channels // members
+
+    def kernel(x_ref, o_ref, sems):
+        copies = []
+        for d in range(members):
+            at = [slice(None)] * len(outer) + [pl.ds(place(d) * width, width)]
+            copies.append(pltpu.make_async_copy(x_ref.at[tuple(at)], o_ref.at[d], sems.at[d]))
+        for copy in copies:
+            copy.start()
+        for copy in copies:
+            copy.wait()
 
     return pl.pallas_call(
         kernel,
-        grid=(tp,),
-        in_specs=[pl.BlockSpec((streams, rows, width), lambda t: (0, 0, t))],
-        out_specs=pl.BlockSpec(
-            (members, 1, per, streams, rows, HEAD_DIM), lambda t: (0, t, 0, 0, 0, 0)
-        ),
-        out_shape=jax.ShapeDtypeStruct((members, tp, per, streams, rows, HEAD_DIM), x.dtype),
+        in_specs=[pl.BlockSpec(memory_space=pl.ANY)],
+        out_specs=pl.BlockSpec(memory_space=pl.ANY),
+        out_shape=jax.ShapeDtypeStruct((members, *outer, width), x.dtype),
+        scratch_shapes=[pltpu.SemaphoreType.DMA((members,))],
         cost_estimate=estimate(0, 4 * x.size),
-        name="pack_qkv",
+        name="split_columns",
     )(x)
 
 
-def unpack_qkv(x, members):
-    _, tp, per, streams, rows, _ = x.shape
-    width = members * per * HEAD_DIM
-
-    def kernel(x_ref, o_ref):
-        for c in range(members):
-            for j in range(per):
-                at = (c * per + j) * HEAD_DIM
-                o_ref[:, :, at : at + HEAD_DIM] = x_ref[c, 0, j]
+def join_columns(x, place):
+    members, *outer, width = x.shape
+
+    def kernel(x_ref, o_ref, sems):
+        copies = []
+        for d in range(members):
+            at = [slice(None)] * len(outer) + [pl.ds(place(d) * width, width)]
+            copies.append(pltpu.make_async_copy(x_ref.at[d], o_ref.at[tuple(at)], sems.at[d]))
+        for copy in copies:
+            copy.start()
+        for copy in copies:
+            copy.wait()
 
     return pl.pallas_call(
         kernel,
-        grid=(tp,),
-        in_specs=[
-            pl.BlockSpec((members, 1, per, streams, rows, HEAD_DIM), lambda t: (0, t, 0, 0, 0, 0))
-        ],
-        out_specs=pl.BlockSpec((streams, rows, width), lambda t: (0, 0, t)),
-        out_shape=jax.ShapeDtypeStruct((streams, rows, tp * width), x.dtype),
+        in_specs=[pl.BlockSpec(memory_space=pl.ANY)],
+        out_specs=pl.BlockSpec(memory_space=pl.ANY),
+        out_shape=jax.ShapeDtypeStruct((*outer, members * width), x.dtype),
+        scratch_shapes=[pltpu.SemaphoreType.DMA((members,))],
         cost_estimate=estimate(0, 4 * x.size),
-        name="unpack_qkv",
-    )(x)
-
-
-def pack_rows(x, members):
-    tokens, width = x.shape
-    per = width // HEAD_DIM // members
-
-    def kernel(x_ref, o_ref):
-        for c in range(members):
-            for j in range(per):
-                at = (c * per + j) * HEAD_DIM
-                o_ref[c, j] = x_ref[:, at : at + HEAD_DIM]
-
-    return pl.pallas_call(
-        kernel,
-        out_shape=jax.ShapeDtypeStruct((members, per, tokens, HEAD_DIM), x.dtype),
-        cost_estimate=estimate(0, 4 * x.size),
-        name="pack_rows",
-    )(x)
-
-
-def unpack_rows(x):
-    members, per, tokens, _ = x.shape
-
-    def kernel(x_ref, o_ref):
-        for c in range(members):
-            for j in range(per):
-                at = (c * per + j) * HEAD_DIM
-                o_ref[:, at : at + HEAD_DIM] = x_ref[c, j]
-
-    return pl.pallas_call(
-        kernel,
-        out_shape=jax.ShapeDtypeStruct((tokens, members * per * HEAD_DIM), x.dtype),
-        cost_estimate=estimate(0, 4 * x.size),
-        name="unpack_rows",
+        name="join_columns",
     )(x)
 
 
@@ -124,11 +90,11 @@
 
 
 def forward_kernel(docs, x_ref, taps_ref, mixed_ref, out_ref, padded):
-    sources, _, streams, rows, _ = x_ref.shape
+    sources, streams, rows, _ = x_ref.shape
     tokens = sources * rows
     padded[:, 0:PAD, :] = jnp.zeros((streams, PAD, HEAD_DIM), jnp.float32)
     for m in range(streams):
-        padded[m, PAD:, :] = x_ref[:, 0, m].reshape(tokens, HEAD_DIM).astype(jnp.float32)
+        padded[m, PAD:, :] = x_ref[:, m].reshape(tokens, HEAD_DIM).astype(jnp.float32)
     for m in range(streams):
         for start in range(0, tokens, BLOCK):
             total = jnp.zeros((BLOCK, HEAD_DIM), jnp.float32)
@@ -144,15 +110,16 @@
             docs, mixed_ref[0, 0, own, :], mixed_ref[0, 1, span, :], block, first
         )
         total = dot(expo.astype(jnp.bfloat16), mixed_ref[0, 2, span, :], ((1,), (0,)))
-        per = out_ref.shape[2]
+        per = out_ref.shape[1]
         at = block * BLOCK
-        out_ref[at // per, 0, at % per : at % per + BLOCK, :] = (total / row_sum).astype(
+        out_ref[at // per, at % per : at % per + BLOCK, :] = (total / row_sum).astype(
             jnp.bfloat16
         )
 
 
 def forward(docs, x, taps, members):
-    sources, per, streams, rows, _ = x.shape
+    sources, streams, rows, width = x.shape
+    per = width // HEAD_DIM
     tokens = sources * rows
     return pl.pallas_call(
         forward_kernel,
@@ -160,18 +127,18 @@
             num_scalar_prefetch=1,
             grid=(per,),
             in_specs=[
-                pl.BlockSpec((sources, 1, streams, rows, HEAD_DIM), lambda h, d: (0, h, 0, 0, 0)),
+                pl.BlockSpec((sources, streams, rows, HEAD_DIM), lambda h, d: (0, 0, 0, h)),
                 pl.BlockSpec((streams, KW, HEAD_DIM), lambda h, d: (0, 0, h)),
             ],
             out_specs=[
                 pl.BlockSpec((1, streams, tokens, HEAD_DIM), lambda h, d: (h, 0, 0, 0)),
-                pl.BlockSpec((members, 1, tokens // members, HEAD_DIM), lambda h, d: (0, h, 0, 0)),
+                pl.BlockSpec((members, tokens // members, HEAD_DIM), lambda h, d: (0, 0, h)),
             ],
             scratch_shapes=[pltpu.VMEM((streams, tokens + PAD, HEAD_DIM), jnp.float32)],
         ),
         out_shape=[
             jax.ShapeDtypeStruct((per, streams, tokens, HEAD_DIM), jnp.bfloat16),
-            jax.ShapeDtypeStruct((members, per, tokens // members, HEAD_DIM), jnp.bfloat16),
+            jax.ShapeDtypeStruct((members, tokens // members, width), jnp.bfloat16),
         ],
         cost_estimate=estimate(10_000_000_000, 8 * x.size),
         name="forward",
@@ -181,9 +148,9 @@
 def backward_kernel(
     docs, x_ref, taps_ref, mixed_ref, att_ref, up_ref, grad_ref, tapg_ref, padded, cgrad
 ):
-    sources, _, streams, rows, _ = x_ref.shape
+    sources, streams, rows, _ = x_ref.shape
     tokens = sources * rows
-    per = att_ref.shape[2]
+    per = att_ref.shape[1]
     cgrad[...] = jnp.zeros_like(cgrad)
     for block in range(tokens // BLOCK):
         first = max(0, block - STEPS)
@@ -195,8 +162,8 @@
             mixed_ref[0, 2, span, :],
         )
         at = block * BLOCK
-        up = up_ref[at // per, 0, at % per : at % per + BLOCK, :]
-        att = att_ref[at // per, 0, at % per : at % per + BLOCK, :]
+        up = up_ref[at // per, at % per : at % per + BLOCK, :]
+        att = att_ref[at // per, at % per : at % per + BLOCK, :]
         delta = jnp.sum(up.astype(jnp.float32) * att.astype(jnp.float32), axis=1, keepdims=True)
         expo, row_sum = masked_scores(docs, query, keys, block, first)
         prob = expo / row_sum
@@ -207,7 +174,7 @@
         cgrad[2, span, :] += dot(prob.astype(jnp.bfloat16), up, ((0,), (0,)))
     padded[:, 0:PAD, :] = jnp.zeros((streams, PAD, HEAD_DIM), jnp.float32)
     for m in range(streams):
-        padded[m, PAD:, :] = x_ref[:, 0, m].reshape(tokens, HEAD_DIM).astype(jnp.float32)
+        padded[m, PAD:, :] = x_ref[:, m].reshape(tokens, HEAD_DIM).astype(jnp.float32)
     for m in range(streams):
         sums = [jnp.zeros((8, HEAD_DIM), jnp.float32) for _ in range(KW)]
         for start in range(0, tokens, BLOCK):
@@ -222,7 +189,7 @@
                 at = PAD + start - lag
                 product = padded[m, at : at + BLOCK, :] * here
                 sums[lag] = sums[lag] + jnp.sum(product.reshape(BLOCK // 8, 8, HEAD_DIM), axis=0)
-            grad_ref[start // rows : (start + BLOCK) // rows, 0, m] = total.astype(
+            grad_ref[start // rows : (start + BLOCK) // rows, m] = total.astype(
                 jnp.bfloat16
             ).reshape(BLOCK // rows, rows, HEAD_DIM)
         for lag in range(KW):
@@ -230,12 +197,13 @@
 
 
 def backward(docs, x, taps, mixed, att, up):
-    sources, per, streams, rows, _ = x.shape
+    sources, streams, rows, width = x.shape
+    per = width // HEAD_DIM
     tokens = sources * rows
     members = att.shape[0]
-    slab = pl.BlockSpec((sources, 1, streams, rows, HEAD_DIM), lambda h, d: (0, h, 0, 0, 0))
+    slab = pl.BlockSpec((sources, streams, rows, HEAD_DIM), lambda h, d: (0, 0, 0, h))
     tap = pl.BlockSpec((streams, KW, HEAD_DIM), lambda h, d: (0, 0, h))
-    rowspec = pl.BlockSpec((members, 1, tokens // members, HEAD_DIM), lambda h, d: (0, h, 0, 0))
+    rowspec = pl.BlockSpec((members, tokens // members, HEAD_DIM), lambda h, d: (0, 0, h))
     return pl.pallas_call(
         backward_kernel,
         grid_spec=pltpu.PrefetchScalarGridSpec(
@@ -266,27 +234,43 @@
 def swap(value, axes):
     shape = value.shape
     return lax.all_to_all(
-        value.reshape(shape[0], -1, HEAD_DIM), axes, split_axis=0, concat_axis=0, tiled=True
+        value.reshape(shape[0], -1, shape[-1]), axes, split_axis=0, concat_axis=0, tiled=True
     ).reshape(shape)
+
+
+def gather_columns(piece):
+    count = lax.axis_size("ctx")
+    position = lax.axis_index("ctx")
+    held, step = piece, 1
+    while step < count:
+        other = lax.ppermute(held, "ctx", [(i, i ^ step) for i in range(count)])
+        low = (position & step) == 0
+        held = jnp.concatenate(
+            [jnp.where(low, held, other), jnp.where(low, other, held)], axis=-1
+        )
+        step *= 2
+    return held
 
 
 def by_heads(qkv, filters, doc_ids, upstream):
     members, tp = lax.axis_size("ctx"), lax.axis_size("tp")
-    rows, streams, _ = qkv.shape
-    per = upstream.shape[1] // HEAD_DIM // members
+    width = upstream.shape[1] // members
     position = lax.axis_index("ctx")
-    packed = pack_qkv(jnp.transpose(qkv, (1, 0, 2)), members)
-    x = swap(packed.reshape((members * tp,) + packed.shape[2:]), AXES)
-    up = swap(pack_rows(upstream, members), "ctx")
-    taps = lax.dynamic_slice_in_dim(filters, position * per * HEAD_DIM, per * HEAD_DIM, 2)
+
+    def column_of(d):
+        return d % tp * members + d // tp
+
+    def same(d):
+        return d
+
+    x = swap(split_columns(jnp.transpose(qkv, (1, 0, 2)), members * tp, column_of), AXES)
+    up = swap(split_columns(upstream, members, same), "ctx")
+    taps = lax.dynamic_slice_in_dim(filters, position * width, width, 2)
     mixed, att = forward(doc_ids, x, taps, members)
-    attended = unpack_rows(swap(att, "ctx"))
+    attended = join_columns(swap(att, "ctx"), same)
     grad, tap_grad = backward(doc_ids, x, taps, mixed, att, up)
-    grad = swap(grad, AXES)
-    qkv_grad = unpack_qkv(grad.reshape((members, tp) + grad.shape[1:]), members)
-    pieces = lax.all_gather(tap_grad, "ctx", axis=0)
-    filter_grad = jnp.transpose(pieces, (1, 2, 0, 3)).reshape(filters.shape)
-    return attended, jnp.transpose(qkv_grad, (1, 0, 2)), filter_grad
+    qkv_grad = join_columns(swap(grad, AXES), column_of)
+    return attended, jnp.transpose(qkv_grad, (1, 0, 2)), gather_columns(tap_grad)
 
 
 def from_behind(value, axis, steps):

time: 158 us -> 248 us (1.57)
  Pallas kernels: 32.7 us -> 154 us
  blocking collectives: 57.9 us -> 0 us
  waiting for transfers between devices: 43.1 us -> 62.9 us
  starting transfers between devices: 19.7 us -> 26.7 us
    pallas_call x4, Pallas kernels: 11.3 us -> 132 us  [the longest x2 66.1 us: split_columns(): pl.pallas_call(kernel, in_specs=[pl.BlockSpec(memory_space=pl.ANY)], out_...]
    all_gather x1 -> x0, blocking collectives: 57.9 us -> none  [by_heads(): pieces = lax.all_gather(tap_grad, 'ctx', axis=0)]
    ppermute x0 -> x3, waiting for transfers between devices: none -> 34.9 us  [gather_columns(): other = lax.ppermute(held, 'ctx', [(i, i ^ step) for i in range(count)])]
    all_to_all x4, waiting for transfers between devices: 43.1 us -> 28 us  [swap(): lax.all_to_all(value.reshape(shape[0], -1, shape[-1]), axes, split_axis=0...]
    ppermute x0 -> x3, starting transfers between devices: none -> 6.99 us  [gather_columns(): other = lax.ppermute(held, 'ctx', [(i, i ^ step) for i in range(count)])]
  transfers between devices with their start and end apart: 4 -> 7, of which waited for: 3 -> 6; matrix products, arithmetic and copies ran while one was open for 1% -> 1% of each run, Pallas kernels for 16% -> 22%
where the time goes in v2:
time: 248 us; the launch traced here: 247 us
  Pallas kernels  154 us (62%)
  waiting for transfers between devices  62.9 us (25%)
  starting transfers between devices  26.7 us (11%)
  local copies, waits for them, and re-layouts  2.59 us (1%)
    pallas_call x2, Pallas kernels, split_columns(): pl.pallas_call(kernel, in_specs=[pl.BlockSpec(memory_space=pl.ANY)], out_...  66.1 us
    pallas_call x2, Pallas kernels, join_columns(): pl.pallas_call(kernel, in_specs=[pl.BlockSpec(memory_space=pl.ANY)], out_...  66.1 us
    ppermute x3, waiting for transfers between devices, gather_columns(): other = lax.ppermute(held, 'ctx', [(i, i ^ step) for i in range(count)])  34.9 us
    all_to_all x4, waiting for transfers between devices, swap(): lax.all_to_all(value.reshape(shape[0], -1, shape[-1]), axes, split_axis=0...  28 us
    all_to_all x4, starting transfers between devices, swap(): lax.all_to_all(value.reshape(shape[0], -1, shape[-1]), axes, split_axis=0...  19.7 us
    pallas_call x1, Pallas kernels, backward(): pl.pallas_call(backward_kernel, grid_spec=pltpu.PrefetchScalarGridSpec(nu...  13.5 us
    pallas_call x1, Pallas kernels, forward(): pl.pallas_call(forward_kernel, grid_spec=pltpu.PrefetchScalarGridSpec(num...  7.81 us
    ppermute x3, starting transfers between devices, gather_columns(): other = lax.ppermute(held, 'ctx', [(i, i ^ step) for i in range(count)])  6.99 us
  transfers between devices with their start and end apart: 7, of which 6 were waited for; matrix products, arithmetic and copies ran while one was open for 1% of the time, Pallas kernels for 22%

profile of v2, /device:TPU:0, one launch (start us, length us, event | category | flops | bytes accessed | tf_op | source)
XLA Modules:
  0.0 247.1 jit_solution(5955193973198666768)
XLA Ops:
  0.6 0.0 copy-start
  0.6 49.0 %split_columns.2 = bf16[32,3,32,256]{3,2,1,0:T(8,128)(2,1)} custom-call(bf16[3,32,8192]{2,1,0:T(8,128)(2,1)} %bitcast.8), custom_call_target="tpu_custom_call" | custom-call | bytes 3145728 | tf_op jit(solution)/shard_map/split_columns/pallas_call | solution.py:39
  49.7 7.3 %all-to-all-start = ((bf16[32,96,256]{2,1,0:T(8,128)(2,1)}), bf16[32,96,256]{2,1,0:T(8,128)(2,1)S(1)}, u32[]{:S(2)}, u32[]{:S(2)}) async-start(bf16[32,96,256]{2,1,0:T(8,128)(2,1)} %bitcast.7), calls=%async_computation | async-start | bytes 3145728 | tf_op jit(solution)/shard_map/all_to_all | solution.py:236
  57.0 17.1 %split_columns.3 = bf16[8,128,256]{2,1,0:T(8,128)(2,1)} custom-call(bf16[128,2048]{1,0:T(8,128)(2,1)} %x_ref.1), custom_call_target="tpu_custom_call" | custom-call | bytes 1048576 | tf_op jit(solution)/shard_map/split_columns/pallas_call | solution.py:39
  74.1 0.0 copy-done
  74.1 0.6 constant_dynamic-slice_fusion.taps_ref
  74.7 20.0 %all-to-all-done = bf16[32,96,256]{2,1,0:T(8,128)(2,1)S(1)} async-done(((bf16[32,96,256]{2,1,0:T(8,128)(2,1)}), bf16[32,96,256]{2,1,0:T(8,128)(2,1)S(1)}, u32[]{:S(2)}, u32[]{:S(2)}) %all-to-all-start) | async-done | bytes 1572896 | tf_op jit(solution)/shard_map/all_to_all | solution.py:236
  94.7 0.0 copy-start.3
  94.7 3.5 %all-to-all-start.2 = ((bf16[8,128,256]{2,1,0:T(8,128)(2,1)}), bf16[8,128,256]{2,1,0:T(8,128)(2,1)S(1)}, u32[]{:S(2)}, u32[]{:S(2)}) async-start(bf16[8,128,256]{2,1,0:T(8,128)(2,1)} %split_columns.3), calls=%async_computation.2 | async-start | bytes 1048576 | tf_op jit(solution)/shard_map/all_to_all | solution.py:236
  98.2 0.0 copy-done.3
  98.2 7.8 %forward.1 = (bf16[2,3,1024,128]{3,2,1,0:T(8,128)(2,1)}, bf16[8,128,256]{2,1,0:T(8,128)(2,1)}) custom-call(s32[8]{0:T(128)} %docs.3, bf16[32,3,32,256]{3,2,1,0:T(8,128)(2,1)} %bitcast.10, f32[3,7,256]{2,1,0:T(8,128)} %constant_dynamic-slice_fusion.taps_ref), custom_call_target="tpu_custom_call" | custom-call | flops 10000000000 | bytes 6291456 | tf_op jit(solution)/shard_map/forward/pallas_call | solution.py:124
  106.1 6.8 %all-to-all-done.2.up_ref = bf16[8,128,256]{2,1,0:T(8,128)(2,1)S(1)} async-done(((bf16[8,128,256]{2,1,0:T(8,128)(2,1)}), bf16[8,128,256]{2,1,0:T(8,128)(2,1)S(1)}, u32[]{:S(2)}, u32[]{:S(2)}) %all-to-all-start.2) | async-done | bytes 524320 | tf_op jit(solution)/shard_map/all_to_all | solution.py:236
  112.9 0.0 copy-start.4
  112.9 3.6 %all-to-all-start.1 = ((bf16[8,128,256]{2,1,0:T(8,128)(2,1)}), bf16[8,128,256]{2,1,0:T(8,128)(2,1)S(1)}, u32[]{:S(2)}, u32[]{:S(2)}) async-start(bf16[8,128,256]{2,1,0:T(8,128)(2,1)} %get-tuple-element.7.att_ref), calls=%async_computation.1 | async-start | bytes 1048576 | tf_op jit(solution)/shard_map/all_to_all | solution.py:236
  116.5 0.0 copy-done.4
  116.5 13.5 %backward.1 = (bf16[32,3,32,256]{3,2,1,0:T(8,128)(2,1)}, f32[3,7,256]{2,1,0:T(8,128)}) custom-call(s32[8]{0:T(128)} %docs.3, bf16[32,3,32,256]{3,2,1,0:T(8,128)(2,1)} %bitcast.11, f32[3,7,256]{2,1,0:T(8,128)} %constant_dynamic-slice_fusion.taps_ref, bf16[2,3,1024,128]{3,2,1,0:T(8,128)(2,1)} %get-tuple-element.8.mixed_ref, ...), custom_call_target="tpu_custom_call" | custom-call | flops 20000000000 | bytes 9437184 | tf_op jit(solution)/shard_map/backward/pallas_call | solution.py:207
  130.0 1.1 all-to-all-done.1.x_ref
  131.2 0.0 copy-start.2
  131.2 0.0 copy-start.5
  131.2 0.8 copy-done.2
  132.0 5.2 %all-to-all-start.3 = ((bf16[32,96,256]{2,1,0:T(8,128)(2,1)}), bf16[32,96,256]{2,1,0:T(8,128)(2,1)S(1)}, u32[]{:S(2)}, u32[]{:S(2)}) async-start(bf16[32,96,256]{2,1,0:T(8,128)(2,1)} %bitcast.9), calls=%async_computation.3 | async-start | bytes 3145728 | tf_op jit(solution)/shard_map/all_to_all | solution.py:236
  137.2 0.0 copy-done.5
  137.2 1.8 collective-permute-start
  139.0 7.0 %collective-permute-done = f32[3,7,256]{2,1,0:T(8,128)S(1)} collective-permute-done((f32[3,7,256]{2,1,0:T(8,128)S(1)}, f32[3,7,256]{2,1,0:T(8,128)S(1)}, u32[]{:S(2)}, u32[]{:S(2)}) %collective-permute-start) | collective-permute-done | bytes 21536 | tf_op jit(solution)/shard_map/ppermute | solution.py:246
  146.1 0.9 collective-permute-start.1
  147.0 17.7 %collective-permute-done.1 = f32[3,7,512]{2,1,0:T(8,128)S(1)} collective-permute-done((f32[3,7,512]{2,1,0:T(8,128)S(1)}, f32[3,7,512]{2,1,0:T(8,128)S(1)}, u32[]{:S(2)}, u32[]{:S(2)}) %collective-permute-start.1) | collective-permute-done | bytes 43040 | tf_op jit(solution)/shard_map/ppermute | solution.py:246
  164.7 4.3 %collective-permute-start.2 = (f32[3,7,1024]{2,1,0:T(8,128)S(1)}, f32[3,7,1024]{2,1,0:T(8,128)S(1)}, u32[]{:S(2)}, u32[]{:S(2)}) collective-permute-start(f32[3,7,1024]{2,1,0:T(8,128)S(1)} %pad_maximum_fusion.1), channel_id=1, source_target_pairs={{0,16},{4,20},{8,24},{12,28},{16,0},{20,4},{24,8},{28,12},{1,17},{... | collective-permute-start | bytes 258056 | tf_op jit(solution)/shard_map/ppermute | solution.py:246
  169.0 10.2 %collective-permute-done.2 = f32[3,7,1024]{2,1,0:T(8,128)S(1)} collective-permute-done((f32[3,7,1024]{2,1,0:T(8,128)S(1)}, f32[3,7,1024]{2,1,0:T(8,128)S(1)}, u32[]{:S(2)}, u32[]{:S(2)}) %collective-permute-start.2) | collective-permute-done | bytes 86048 | tf_op jit(solution)/shard_map/ppermute | solution.py:246
  179.2 0.7 pad_maximum_fusion
  179.9 17.1 %join_columns.2 = bf16[128,2048]{1,0:T(8,128)(2,1)} custom-call(bf16[8,128,256]{2,1,0:T(8,128)(2,1)} %copy-done.2), custom_call_target="tpu_custom_call" | custom-call | bytes 1048576 | tf_op jit(solution)/shard_map/join_columns/pallas_call | solution.py:63
  196.9 0.0 all-to-all-done.3
  196.9 0.0 copy-start.1
  196.9 1.2 copy-done.1
  198.1 49.0 %join_columns.3 = bf16[3,32,8192]{2,1,0:T(8,128)(2,1)} custom-call(bf16[32,3,32,256]{3,2,1,0:T(8,128)(2,1)} %bitcast.6), custom_call_target="tpu_custom_call" | custom-call | bytes 3145728 | tf_op jit(solution)/shard_map/join_columns/pallas_call | solution.py:63
  (5 shorter events, 0.1 us)
Async XLA Ops:
  0.6 73.4 %copy-start = (f32[3,7,2048]{2,1,0:T(8,128)S(1)}, f32[3,7,2048]{2,1,0:T(8,128)}, u32[]{:S(2)}) copy-start(f32[3,7,2048]{2,1,0:T(8,128)} %param.5) | copy-start | bytes 516100
  49.7 45.0 %all-to-all-start = ((bf16[32,96,256]{2,1,0:T(8,128)(2,1)}), bf16[32,96,256]{2,1,0:T(8,128)(2,1)S(1)}, u32[]{:S(2)}, u32[]{:S(2)}) async-start(bf16[32,96,256]{2,1,0:T(8,128)(2,1)} %bitcast.7), calls=%async_computation | async-start | bytes 3145728 | tf_op jit(solution)/shard_map/all_to_all | solution.py:236
  94.7 3.5 %copy-start.3 = (bf16[32,96,256]{2,1,0:T(8,128)(2,1)}, bf16[32,96,256]{2,1,0:T(8,128)(2,1)S(1)}, u32[]{:S(2)}) copy-start(bf16[32,96,256]{2,1,0:T(8,128)(2,1)S(1)} %all-to-all-done) | copy-start | bytes 4718596
  94.7 18.1 %all-to-all-start.2 = ((bf16[8,128,256]{2,1,0:T(8,128)(2,1)}), bf16[8,128,256]{2,1,0:T(8,128)(2,1)S(1)}, u32[]{:S(2)}, u32[]{:S(2)}) async-start(bf16[8,128,256]{2,1,0:T(8,128)(2,1)} %split_columns.3), calls=%async_computation.2 | async-start | bytes 1048576 | tf_op jit(solution)/shard_map/all_to_all | solution.py:236
  112.9 3.6 %copy-start.4 = (bf16[8,128,256]{2,1,0:T(8,128)(2,1)}, bf16[8,128,256]{2,1,0:T(8,128)(2,1)S(1)}, u32[]{:S(2)}) copy-start(bf16[8,128,256]{2,1,0:T(8,128)(2,1)S(1)} %all-to-all-done.2.up_ref) | copy-start | bytes 1572868
  112.9 18.3 %all-to-all-start.1 = ((bf16[8,128,256]{2,1,0:T(8,128)(2,1)}), bf16[8,128,256]{2,1,0:T(8,128)(2,1)S(1)}, u32[]{:S(2)}, u32[]{:S(2)}) async-start(bf16[8,128,256]{2,1,0:T(8,128)(2,1)} %get-tuple-element.7.att_ref), calls=%async_computation.1 | async-start | bytes 1048576 | tf_op jit(solution)/shard_map/all_to_all | solution.py:236
  131.2 0.8 copy-start.2
  131.2 6.0 %copy-start.5 = (f32[3,7,256]{2,1,0:T(8,128)S(1)}, f32[3,7,256]{2,1,0:T(8,128)}, u32[]{:S(2)}) copy-start(f32[3,7,256]{2,1,0:T(8,128)} %get-tuple-element.10) | copy-start | bytes 64516
  132.0 65.0 %all-to-all-start.3 = ((bf16[32,96,256]{2,1,0:T(8,128)(2,1)}), bf16[32,96,256]{2,1,0:T(8,128)(2,1)S(1)}, u32[]{:S(2)}, u32[]{:S(2)}) async-start(bf16[32,96,256]{2,1,0:T(8,128)(2,1)} %bitcast.9), calls=%async_computation.3 | async-start | bytes 3145728 | tf_op jit(solution)/shard_map/all_to_all | solution.py:236
  137.2 8.9 %collective-permute-start = (f32[3,7,256]{2,1,0:T(8,128)S(1)}, f32[3,7,256]{2,1,0:T(8,128)S(1)}, u32[]{:S(2)}, u32[]{:S(2)}) collective-permute-start(f32[3,7,256]{2,1,0:T(8,128)S(1)} %copy-done.5), channel_id=1, source_target_pairs={{0,4},{4,0},{8,12},{12,8},{16,20},{20,16},{24,28},{28,24},{1,5},{5... | collective-permute-start | bytes 64520 | tf_op jit(solution)/shard_map/ppermute | solution.py:246
  146.1 18.5 %collective-permute-start.1 = (f32[3,7,512]{2,1,0:T(8,128)S(1)}, f32[3,7,512]{2,1,0:T(8,128)S(1)}, u32[]{:S(2)}, u32[]{:S(2)}) collective-permute-start(f32[3,7,512]{2,1,0:T(8,128)S(1)} %pad_maximum_fusion.2), channel_id=1, source_target_pairs={{0,8},{4,12},{8,0},{12,4},{16,24},{20,28},{24,16},{28,20},{1,9},{5... | collective-permute-start | bytes 129032 | tf_op jit(solution)/shard_map/ppermute | solution.py:246
  164.7 14.5 %collective-permute-start.2 = (f32[3,7,1024]{2,1,0:T(8,128)S(1)}, f32[3,7,1024]{2,1,0:T(8,128)S(1)}, u32[]{:S(2)}, u32[]{:S(2)}) collective-permute-start(f32[3,7,1024]{2,1,0:T(8,128)S(1)} %pad_maximum_fusion.1), channel_id=1, source_target_pairs={{0,16},{4,20},{8,24},{12,28},{16,0},{20,4},{24,8},{28,12},{1,17},{... | collective-permute-start | bytes 258056 | tf_op jit(solution)/shard_map/ppermute | solution.py:246
  196.9 1.2 copy-start.1

commit v3 on v2

--- a/solution.py
+++ b/solution.py
@@ -22,50 +22,46 @@
     return pl.CostEstimate(flops=flops, bytes_accessed=moved, transcendentals=0)
 
 
-def split_columns(x, members, place):
-    *outer, channels = x.shape
-    width = channels // members
-
-    def kernel(x_ref, o_ref, sems):
-        copies = []
-        for d in range(members):
-            at = [slice(None)] * len(outer) + [pl.ds(place(d) * width, width)]
-            copies.append(pltpu.make_async_copy(x_ref.at[tuple(at)], o_ref.at[d], sems.at[d]))
-        for copy in copies:
-            copy.start()
-        for copy in copies:
-            copy.wait()
+def split_columns(x, members, tp):
+    streams, rows, channels = x.shape
+    width = channels // tp // members
+    steps = 2 if tp % 2 == 0 else 1
+    part = tp // steps
+
+    def kernel(x_ref, o_ref):
+        for t in range(part):
+            for c in range(members):
+                at = (t * members + c) * width
+                o_ref[c, t] = x_ref[:, :, at : at + width]
 
     return pl.pallas_call(
         kernel,
-        in_specs=[pl.BlockSpec(memory_space=pl.ANY)],
-        out_specs=pl.BlockSpec(memory_space=pl.ANY),
-        out_shape=jax.ShapeDtypeStruct((members, *outer, width), x.dtype),
-        scratch_shapes=[pltpu.SemaphoreType.DMA((members,))],
+        grid=(steps,),
+        in_specs=[pl.BlockSpec((streams, rows, part * members * width), lambda i: (0, 0, i))],
+        out_specs=pl.BlockSpec((members, part, streams, rows, width), lambda i: (0, i, 0, 0, 0)),
+        out_shape=jax.ShapeDtypeStruct((members, tp, streams, rows, width), x.dtype),
         cost_estimate=estimate(0, 4 * x.size),
         name="split_columns",
     )(x)
 
 
-def join_columns(x, place):
-    members, *outer, width = x.shape
-
-    def kernel(x_ref, o_ref, sems):
-        copies = []
-        for d in range(members):
-            at = [slice(None)] * len(outer) + [pl.ds(place(d) * width, width)]
-            copies.append(pltpu.make_async_copy(x_ref.at[d], o_ref.at[tuple(at)], sems.at[d]))
-        for copy in copies:
-            copy.start()
-        for copy in copies:
-            copy.wait()
+def join_columns(x):
+    members, tp, streams, rows, width = x.shape
+    steps = 2 if tp % 2 == 0 else 1
+    part = tp // steps
+
+    def kernel(x_ref, o_ref):
+        for t in range(part):
+            for c in range(members):
+                at = (t * members + c) * width
+                o_ref[:, :, at : at + width] = x_ref[c, t]
 
     return pl.pallas_call(
         kernel,
-        in_specs=[pl.BlockSpec(memory_space=pl.ANY)],
-        out_specs=pl.BlockSpec(memory_space=pl.ANY),
-        out_shape=jax.ShapeDtypeStruct((*outer, members * width), x.dtype),
-        scratch_shapes=[pltpu.SemaphoreType.DMA((members,))],
+        grid=(steps,),
+        in_specs=[pl.BlockSpec((members, part, streams, rows, width), lambda i: (0, i, 0, 0, 0))],
+        out_specs=pl.BlockSpec((streams, rows, part * members * width), lambda i: (0, 0, i)),
+        out_shape=jax.ShapeDtypeStruct((streams, rows, tp * members * width), x.dtype),
         cost_estimate=estimate(0, 4 * x.size),
         name="join_columns",
     )(x)
@@ -238,39 +234,51 @@
     ).reshape(shape)
 
 
-def gather_columns(piece):
+def gather_columns(piece, members):
     count = lax.axis_size("ctx")
-    position = lax.axis_index("ctx")
-    held, step = piece, 1
-    while step < count:
-        other = lax.ppermute(held, "ctx", [(i, i ^ step) for i in range(count)])
-        low = (position & step) == 0
-        held = jnp.concatenate(
-            [jnp.where(low, held, other), jnp.where(low, other, held)], axis=-1
-        )
-        step *= 2
-    return held
+    streams, taps, width = piece.shape
+    pieces = [piece]
+    for step in range(1, count):
+        pieces.append(lax.ppermute(piece, "ctx", [(i, i ^ step) for i in range(count)]))
+    position = lax.axis_index("ctx").astype(jnp.int32).reshape(1)
+
+    def kernel(position_ref, *refs):
+        o_ref = refs[-1]
+        for step in range(members):
+            column = lax.rem(position_ref[0] ^ step, members)
+            at = pl.multiple_of(column * width, width)
+            total = refs[step][...]
+            for other in range(step + members, count, members):
+                total = total + refs[other][...]
+            o_ref[:, :, pl.ds(at, width)] = total
+
+    whole = pl.BlockSpec((streams, taps, width), lambda i, p: (0, 0, 0))
+    return pl.pallas_call(
+        kernel,
+        grid_spec=pltpu.PrefetchScalarGridSpec(
+            num_scalar_prefetch=1,
+            grid=(1,),
+            in_specs=[whole] * count,
+            out_specs=pl.BlockSpec((streams, taps, members * width), lambda i, p: (0, 0, 0)),
+        ),
+        out_shape=jax.ShapeDtypeStruct((streams, taps, members * width), piece.dtype),
+        name="place_columns",
+    )(position, *pieces)
 
 
 def by_heads(qkv, filters, doc_ids, upstream):
     members, tp = lax.axis_size("ctx"), lax.axis_size("tp")
     width = upstream.shape[1] // members
     position = lax.axis_index("ctx")
-
-    def column_of(d):
-        return d % tp * members + d // tp
-
-    def same(d):
-        return d
-
-    x = swap(split_columns(jnp.transpose(qkv, (1, 0, 2)), members * tp, column_of), AXES)
-    up = swap(split_columns(upstream, members, same), "ctx")
+    slabs = split_columns(jnp.transpose(qkv, (1, 0, 2)), members, tp)
+    x = swap(slabs.reshape((members * tp,) + slabs.shape[2:]), AXES)
+    up = swap(split_columns(upstream[None], members, 1)[:, 0, 0], "ctx")
     taps = lax.dynamic_slice_in_dim(filters, position * width, width, 2)
     mixed, att = forward(doc_ids, x, taps, members)
-    attended = join_columns(swap(att, "ctx"), same)
+    attended = join_columns(swap(att, "ctx")[:, None, None])[0]
     grad, tap_grad = backward(doc_ids, x, taps, mixed, att, up)
-    qkv_grad = join_columns(swap(grad, AXES), column_of)
-    return attended, jnp.transpose(qkv_grad, (1, 0, 2)), gather_columns(tap_grad)
+    qkv_grad = join_columns(swap(grad, AXES).reshape(slabs.shape))
+    return attended, jnp.transpose(qkv_grad, (1, 0, 2)), gather_columns(tap_grad, members)
 
 
 def from_behind(value, axis, steps):
@@ -386,7 +394,8 @@
     def shards(qkv, filters, doc_ids, upstream):
         heads = upstream.shape[1] // HEAD_DIM
         tokens = upstream.shape[0]
-        whole = heads % mesh.shape["ctx"] == 0 and tokens % BLOCK == 0
+        count = mesh.shape["ctx"]
+        whole = heads % count == 0 and tokens % BLOCK == 0 and count & (count - 1) == 0
         form = by_heads if whole else by_ring
         return form(qkv, filters, doc_ids, upstream)
 

time: 248 us -> 145 us (0.58)
  Pallas kernels: 154 us -> 31.4 us
  starting transfers between devices: 26.7 us -> 40.4 us
  waiting for transfers between devices: 62.9 us -> 68.3 us
    pallas_call x4 -> x5, Pallas kernels: 132 us -> 10 us  [the longest x2 4.26 us: split_columns(): pl.pallas_call(kernel, grid=(steps,), in_specs=[pl.BlockSpec((streams, ro...]
    all_to_all x4, waiting for transfers between devices: 28 us -> 43.1 us  [swap(): lax.all_to_all(value.reshape(shape[0], -1, shape[-1]), axes, split_axis=0...]
    ppermute x3 -> x7, starting transfers between devices: 6.99 us -> 20.7 us  [gather_columns(): lax.ppermute(piece, 'ctx', [(i, i ^ step) for i in range(count)])]
    ppermute x3 -> x7, waiting for transfers between devices: 34.9 us -> 25.2 us  [gather_columns(): lax.ppermute(piece, 'ctx', [(i, i ^ step) for i in range(count)])]
  transfers between devices with their start and end apart: 7 -> 11, of which waited for: 6 -> 6; matrix products, arithmetic and copies ran while one was open for 1% -> 0% of each run, Pallas kernels for 22% -> 19%
where the time goes in v3:
time: 145 us; the launch traced here: 144 us
  waiting for transfers between devices  68.3 us (47%)
  starting transfers between devices  40.4 us (28%)
  Pallas kernels  31.4 us (22%)
  local copies, waits for them, and re-layouts  3.2 us (2%)
    all_to_all x4, waiting for transfers between devices, swap(): lax.all_to_all(value.reshape(shape[0], -1, shape[-1]), axes, split_axis=0...  43.1 us
    ppermute x7, waiting for transfers between devices, gather_columns(): lax.ppermute(piece, 'ctx', [(i, i ^ step) for i in range(count)])  25.2 us
    ppermute x7, starting transfers between devices, gather_columns(): lax.ppermute(piece, 'ctx', [(i, i ^ step) for i in range(count)])  20.7 us
    all_to_all x4, starting transfers between devices, swap(): lax.all_to_all(value.reshape(shape[0], -1, shape[-1]), axes, split_axis=0...  19.7 us
    pallas_call x1, Pallas kernels, backward(): pl.pallas_call(backward_kernel, grid_spec=pltpu.PrefetchScalarGridSpec(nu...  13.6 us
    pallas_call x1, Pallas kernels, forward(): pl.pallas_call(forward_kernel, grid_spec=pltpu.PrefetchScalarGridSpec(num...  7.81 us
    pallas_call x2, Pallas kernels, split_columns(): pl.pallas_call(kernel, grid=(steps,), in_specs=[pl.BlockSpec((streams, ro...  4.26 us
    pallas_call x2, Pallas kernels, join_columns(): pl.pallas_call(kernel, grid=(steps,), in_specs=[pl.BlockSpec((members, pa...  4.23 us
  transfers between devices with their start and end apart: 11, of which 6 were waited for; matrix products, arithmetic and copies ran while one was open for 0% of the time, Pallas kernels for 19%

profile of v3, /device:TPU:0, one launch (start us, length us, event | category | flops | bytes accessed | tf_op | source)
XLA Modules:
  0.0 144.1 jit_solution(16900953284376869688)
XLA Ops:
  0.6 0.0 copy-start
  0.6 2.4 %split_columns.2 = bf16[8,4,3,32,256]{4,3,2,1,0:T(8,128)(2,1)} custom-call(bf16[3,32,8192]{2,1,0:T(8,128)(2,1)} %bitcast.15), custom_call_target="tpu_custom_call" | custom-call | bytes 3145728 | tf_op jit(solution)/shard_map/split_columns/pallas_call | solution.py:37
  3.0 7.3 %all-to-all-start = ((bf16[32,96,256]{2,1,0:T(8,128)(2,1)}), bf16[32,96,256]{2,1,0:T(8,128)(2,1)S(1)}, u32[]{:S(2)}, u32[]{:S(2)}) async-start(bf16[32,96,256]{2,1,0:T(8,128)(2,1)} %bitcast.12), calls=%async_computation | async-start | bytes 3145728 | tf_op jit(solution)/shard_map/all_to_all | solution.py:232
  10.3 1.9 %split_columns.3 = bf16[8,1,1,128,256]{4,3,2,1,0:T(8,128)(2,1)} custom-call(bf16[1,128,2048]{2,1,0:T(8,128)(2,1)} %bitcast.20), custom_call_target="tpu_custom_call" | custom-call | bytes 1048576 | tf_op jit(solution)/shard_map/split_columns/pallas_call | solution.py:37
  12.2 0.0 copy-done
  12.2 0.6 constant_dynamic-slice_fusion.taps_ref
  12.8 35.2 %all-to-all-done = bf16[32,96,256]{2,1,0:T(8,128)(2,1)S(1)} async-done(((bf16[32,96,256]{2,1,0:T(8,128)(2,1)}), bf16[32,96,256]{2,1,0:T(8,128)(2,1)S(1)}, u32[]{:S(2)}, u32[]{:S(2)}) %all-to-all-start) | async-done | bytes 1572896 | tf_op jit(solution)/shard_map/all_to_all | solution.py:232
  48.1 3.5 %all-to-all-start.2 = ((bf16[8,128,256]{2,1,0:T(8,128)(2,1)}), bf16[8,128,256]{2,1,0:T(8,128)(2,1)S(1)}, u32[]{:S(2)}, u32[]{:S(2)}) async-start(bf16[8,128,256]{2,1,0:T(8,128)(2,1)} %bitcast.14), calls=%async_computation.2 | async-start | bytes 1048576 | tf_op jit(solution)/shard_map/all_to_all | solution.py:232
  51.6 0.0 copy-done.3
  51.6 7.8 %forward.1 = (bf16[2,3,1024,128]{3,2,1,0:T(8,128)(2,1)}, bf16[8,128,256]{2,1,0:T(8,128)(2,1)}) custom-call(s32[8]{0:T(128)} %docs.3, bf16[32,3,32,256]{3,2,1,0:T(8,128)(2,1)} %bitcast.17, f32[3,7,256]{2,1,0:T(8,128)} %constant_dynamic-slice_fusion.taps_ref), custom_call_target="tpu_custom_call" | custom-call | flops 10000000000 | bytes 6291456 | tf_op jit(solution)/shard_map/forward/pallas_call | solution.py:120
  59.4 6.8 %all-to-all-done.2.up_ref = bf16[8,128,256]{2,1,0:T(8,128)(2,1)S(1)} async-done(((bf16[8,128,256]{2,1,0:T(8,128)(2,1)}), bf16[8,128,256]{2,1,0:T(8,128)(2,1)S(1)}, u32[]{:S(2)}, u32[]{:S(2)}) %all-to-all-start.2) | async-done | bytes 524320 | tf_op jit(solution)/shard_map/all_to_all | solution.py:232
  66.2 0.0 copy-start.4
  66.2 3.6 %all-to-all-start.1 = ((bf16[8,128,256]{2,1,0:T(8,128)(2,1)}), bf16[8,128,256]{2,1,0:T(8,128)(2,1)S(1)}, u32[]{:S(2)}, u32[]{:S(2)}) async-start(bf16[8,128,256]{2,1,0:T(8,128)(2,1)} %get-tuple-element.7.att_ref), calls=%async_computation.1 | async-start | bytes 1048576 | tf_op jit(solution)/shard_map/all_to_all | solution.py:232
  69.8 0.0 copy-done.4
  69.8 13.6 %backward.1 = (bf16[32,3,32,256]{3,2,1,0:T(8,128)(2,1)}, f32[3,7,256]{2,1,0:T(8,128)}) custom-call(s32[8]{0:T(128)} %docs.3, bf16[32,3,32,256]{3,2,1,0:T(8,128)(2,1)} %bitcast.18, f32[3,7,256]{2,1,0:T(8,128)} %constant_dynamic-slice_fusion.taps_ref, bf16[2,3,1024,128]{3,2,1,0:T(8,128)(2,1)} %get-tuple-element.8.mixed_ref, ...), custom_call_target="tpu_custom_call" | custom-call | flops 20000000000 | bytes 9437184 | tf_op jit(solution)/shard_map/backward/pallas_call | solution.py:203
  83.4 1.1 all-to-all-done.1
  84.5 0.0 copy-start.2
  84.5 0.8 copy-done.2
  85.3 5.3 %all-to-all-start.3 = ((bf16[32,96,256]{2,1,0:T(8,128)(2,1)}), bf16[32,96,256]{2,1,0:T(8,128)(2,1)S(1)}, u32[]{:S(2)}, u32[]{:S(2)}) async-start(bf16[32,96,256]{2,1,0:T(8,128)(2,1)} %bitcast.16), calls=%async_computation.3 | async-start | bytes 3145728 | tf_op jit(solution)/shard_map/all_to_all | solution.py:232
  90.6 0.0 copy-done.5
  90.6 4.6 %collective-permute-start.6 = (f32[3,7,256]{2,1,0:T(8,128)S(1)}, f32[3,7,256]{2,1,0:T(8,128)S(1)}, u32[]{:S(2)}, u32[]{:S(2)}) collective-permute-start(f32[3,7,256]{2,1,0:T(8,128)S(1)} %copy-done.5), channel_id=1, source_target_pairs={{0,28},{4,24},{8,20},{12,16},{16,12},{20,8},{24,4},{28,0},{1,29},{... | collective-permute-start | bytes 64520 | tf_op jit(solution)/shard_map/ppermute | solution.py:242
  95.2 0.5 collective-permute-start.5
  95.7 0.6 collective-permute-start.4
  96.2 2.0 %collective-permute-start.3 = (f32[3,7,256]{2,1,0:T(8,128)S(1)}, f32[3,7,256]{2,1,0:T(8,128)S(1)}, u32[]{:S(2)}, u32[]{:S(2)}) collective-permute-start(f32[3,7,256]{2,1,0:T(8,128)S(1)} %copy-done.5), channel_id=1, source_target_pairs={{0,16},{4,20},{8,24},{12,28},{16,0},{20,4},{24,8},{28,12},{1,17},{... | collective-permute-start | bytes 64520 | tf_op jit(solution)/shard_map/ppermute | solution.py:242
  98.3 2.2 %collective-permute-start.2 = (f32[3,7,256]{2,1,0:T(8,128)S(1)}, f32[3,7,256]{2,1,0:T(8,128)S(1)}, u32[]{:S(2)}, u32[]{:S(2)}) collective-permute-start(f32[3,7,256]{2,1,0:T(8,128)S(1)} %copy-done.5), channel_id=1, source_target_pairs={{0,12},{4,8},{8,4},{12,0},{16,28},{20,24},{24,20},{28,16},{1,13},{... | collective-permute-start | bytes 64520 | tf_op jit(solution)/shard_map/ppermute | solution.py:242
  100.5 22.2 %collective-permute-done.6.refs_7_ = f32[3,7,256]{2,1,0:T(8,128)S(1)} collective-permute-done((f32[3,7,256]{2,1,0:T(8,128)S(1)}, f32[3,7,256]{2,1,0:T(8,128)S(1)}, u32[]{:S(2)}, u32[]{:S(2)}) %collective-permute-start.6) | collective-permute-done | bytes 21536 | tf_op jit(solution)/shard_map/ppermute | solution.py:242
  122.7 10.0 %collective-permute-start.1 = (f32[3,7,256]{2,1,0:T(8,128)S(1)}, f32[3,7,256]{2,1,0:T(8,128)S(1)}, u32[]{:S(2)}, u32[]{:S(2)}) collective-permute-start(f32[3,7,256]{2,1,0:T(8,128)S(1)} %copy-done.5), channel_id=1, source_target_pairs={{0,8},{4,12},{8,0},{12,4},{16,24},{20,28},{24,16},{28,20},{1,9},{5... | collective-permute-start | bytes 64520 | tf_op jit(solution)/shard_map/ppermute | solution.py:242
  132.6 0.0 collective-permute-done.5.refs_6_
  132.7 0.8 collective-permute-start
  133.4 0.0 collective-permute-done.4.refs_5_
  133.4 0.0 collective-permute-done.3.refs_4_
  133.4 0.0 copy-start.9
  133.5 0.0 collective-permute-done.2.refs_3_
  133.5 0.0 copy-start.10
  133.5 1.0 collective-permute-done.1.refs_2_
  134.5 2.0 %collective-permute-done.refs_1_ = f32[3,7,256]{2,1,0:T(8,128)S(1)} collective-permute-done((f32[3,7,256]{2,1,0:T(8,128)S(1)}, f32[3,7,256]{2,1,0:T(8,128)S(1)}, u32[]{:S(2)}, u32[]{:S(2)}) %collective-permute-start) | collective-permute-done | bytes 21536 | tf_op jit(solution)/shard_map/ppermute | solution.py:242
  136.5 0.0 copy-done.6
  136.5 0.0 copy-done.7
  136.5 0.0 copy-done.8
  136.5 0.0 copy-done.9
  136.5 0.0 copy-done.10
  136.5 0.0 copy-done.11
  136.5 0.6 copy-done.12
  137.1 1.6 %place_columns.1 = f32[3,7,2048]{2,1,0:T(8,128)} custom-call(s32[1]{0:T(128)} %bitcast.10.position_ref, f32[3,7,256]{2,1,0:T(8,128)} %get-tuple-element.10.refs_0_, f32[3,7,256]{2,1,0:T(8,128)} %copy-done.12, f32[3,7,256]{2,1,0:T(8,128)} %copy-done.11, f32[3,7,256]{2,1,0:T(8,128)} %copy-done.10, f32[3,7,256]{2,1,0:T(8,128)} %copy-done.9, ...), custom_call_target="tpu_custom_call" | custom-call | tf_op jit(solution)/shard_map/place_columns/pallas_call | solution.py:256
  138.7 1.9 %join_columns.2 = bf16[1,128,2048]{2,1,0:T(8,128)(2,1)} custom-call(bf16[8,1,1,128,256]{4,3,2,1,0:T(8,128)(2,1)} %bitcast.13), custom_call_target="tpu_custom_call" | custom-call | bytes 1048576 | tf_op jit(solution)/shard_map/join_columns/pallas_call | solution.py:59
  140.5 0.0 all-to-all-done.3
  140.5 1.2 copy-done.1
  141.7 2.3 %join_columns.3 = bf16[3,32,8192]{2,1,0:T(8,128)(2,1)} custom-call(bf16[8,4,3,32,256]{4,3,2,1,0:T(8,128)(2,1)} %bitcast.11), custom_call_target="tpu_custom_call" | custom-call | bytes 3145728 | tf_op jit(solution)/shard_map/join_columns/pallas_call | solution.py:59
  (8 shorter events, 0.0 us)
Async XLA Ops:
  0.6 11.6 %copy-start = (f32[3,7,2048]{2,1,0:T(8,128)S(1)}, f32[3,7,2048]{2,1,0:T(8,128)}, u32[]{:S(2)}) copy-start(f32[3,7,2048]{2,1,0:T(8,128)} %param.5) | copy-start | bytes 516100
  3.0 45.0 %all-to-all-start = ((bf16[32,96,256]{2,1,0:T(8,128)(2,1)}), bf16[32,96,256]{2,1,0:T(8,128)(2,1)S(1)}, u32[]{:S(2)}, u32[]{:S(2)}) async-start(bf16[32,96,256]{2,1,0:T(8,128)(2,1)} %bitcast.12), calls=%async_computation | async-start | bytes 3145728 | tf_op jit(solution)/shard_map/all_to_all | solution.py:232
  48.1 3.5 %copy-start.3 = (bf16[32,96,256]{2,1,0:T(8,128)(2,1)}, bf16[32,96,256]{2,1,0:T(8,128)(2,1)S(1)}, u32[]{:S(2)}) copy-start(bf16[32,96,256]{2,1,0:T(8,128)(2,1)S(1)} %all-to-all-done) | copy-start | bytes 4718596
  48.1 18.1 %all-to-all-start.2 = ((bf16[8,128,256]{2,1,0:T(8,128)(2,1)}), bf16[8,128,256]{2,1,0:T(8,128)(2,1)S(1)}, u32[]{:S(2)}, u32[]{:S(2)}) async-start(bf16[8,128,256]{2,1,0:T(8,128)(2,1)} %bitcast.14), calls=%async_computation.2 | async-start | bytes 1048576 | tf_op jit(solution)/shard_map/all_to_all | solution.py:232
  66.2 3.6 %copy-start.4 = (bf16[8,128,256]{2,1,0:T(8,128)(2,1)}, bf16[8,128,256]{2,1,0:T(8,128)(2,1)S(1)}, u32[]{:S(2)}) copy-start(bf16[8,128,256]{2,1,0:T(8,128)(2,1)S(1)} %all-to-all-done.2.up_ref) | copy-start | bytes 1572868
  66.2 18.3 %all-to-all-start.1 = ((bf16[8,128,256]{2,1,0:T(8,128)(2,1)}), bf16[8,128,256]{2,1,0:T(8,128)(2,1)S(1)}, u32[]{:S(2)}, u32[]{:S(2)}) async-start(bf16[8,128,256]{2,1,0:T(8,128)(2,1)} %get-tuple-element.7.att_ref), calls=%async_computation.1 | async-start | bytes 1048576 | tf_op jit(solution)/shard_map/all_to_all | solution.py:232
  84.5 0.8 copy-start.2
  84.5 6.1 %copy-start.5 = (f32[3,7,256]{2,1,0:T(8,128)S(1)}, f32[3,7,256]{2,1,0:T(8,128)}, u32[]{:S(2)}) copy-start(f32[3,7,256]{2,1,0:T(8,128)} %get-tuple-element.10.refs_0_) | copy-start | bytes 64516
  85.3 55.3 %all-to-all-start.3 = ((bf16[32,96,256]{2,1,0:T(8,128)(2,1)}), bf16[32,96,256]{2,1,0:T(8,128)(2,1)S(1)}, u32[]{:S(2)}, u32[]{:S(2)}) async-start(bf16[32,96,256]{2,1,0:T(8,128)(2,1)} %bitcast.16), calls=%async_computation.3 | async-start | bytes 3145728 | tf_op jit(solution)/shard_map/all_to_all | solution.py:232
  90.6 32.1 %collective-permute-start.6 = (f32[3,7,256]{2,1,0:T(8,128)S(1)}, f32[3,7,256]{2,1,0:T(8,128)S(1)}, u32[]{:S(2)}, u32[]{:S(2)}) collective-permute-start(f32[3,7,256]{2,1,0:T(8,128)S(1)} %copy-done.5), channel_id=1, source_target_pairs={{0,28},{4,24},{8,20},{12,16},{16,12},{20,8},{24,4},{28,0},{1,29},{... | collective-permute-start | bytes 64520 | tf_op jit(solution)/shard_map/ppermute | solution.py:242
  95.2 37.5 %collective-permute-start.5 = (f32[3,7,256]{2,1,0:T(8,128)S(1)}, f32[3,7,256]{2,1,0:T(8,128)S(1)}, u32[]{:S(2)}, u32[]{:S(2)}) collective-permute-start(f32[3,7,256]{2,1,0:T(8,128)S(1)} %copy-done.5), channel_id=1, source_target_pairs={{0,24},{4,28},{8,16},{12,20},{16,8},{20,12},{24,0},{28,4},{1,25},{... | collective-permute-start | bytes 64520 | tf_op jit(solution)/shard_map/ppermute | solution.py:242
  95.7 37.8 %collective-permute-start.4 = (f32[3,7,256]{2,1,0:T(8,128)S(1)}, f32[3,7,256]{2,1,0:T(8,128)S(1)}, u32[]{:S(2)}, u32[]{:S(2)}) collective-permute-start(f32[3,7,256]{2,1,0:T(8,128)S(1)} %copy-done.5), channel_id=1, source_target_pairs={{0,20},{4,16},{8,28},{12,24},{16,4},{20,0},{24,12},{28,8},{1,21},{... | collective-permute-start | bytes 64520 | tf_op jit(solution)/shard_map/ppermute | solution.py:242
  96.2 37.2 %collective-permute-start.3 = (f32[3,7,256]{2,1,0:T(8,128)S(1)}, f32[3,7,256]{2,1,0:T(8,128)S(1)}, u32[]{:S(2)}, u32[]{:S(2)}) collective-permute-start(f32[3,7,256]{2,1,0:T(8,128)S(1)} %copy-done.5), channel_id=1, source_target_pairs={{0,16},{4,20},{8,24},{12,28},{16,0},{20,4},{24,8},{28,12},{1,17},{... | collective-permute-start | bytes 64520 | tf_op jit(solution)/shard_map/ppermute | solution.py:242
  98.3 35.2 %collective-permute-start.2 = (f32[3,7,256]{2,1,0:T(8,128)S(1)}, f32[3,7,256]{2,1,0:T(8,128)S(1)}, u32[]{:S(2)}, u32[]{:S(2)}) collective-permute-start(f32[3,7,256]{2,1,0:T(8,128)S(1)} %copy-done.5), channel_id=1, source_target_pairs={{0,12},{4,8},{8,4},{12,0},{16,28},{20,24},{24,20},{28,16},{1,13},{... | collective-permute-start | bytes 64520 | tf_op jit(solution)/shard_map/ppermute | solution.py:242
  122.7 13.8 %copy-start.6 = (f32[3,7,256]{2,1,0:T(8,128)}, f32[3,7,256]{2,1,0:T(8,128)S(1)}, u32[]{:S(2)}) copy-start(f32[3,7,256]{2,1,0:T(8,128)S(1)} %collective-permute-done.6.refs_7_) | copy-start | bytes 64516
  122.7 11.8 %collective-permute-start.1 = (f32[3,7,256]{2,1,0:T(8,128)S(1)}, f32[3,7,256]{2,1,0:T(8,128)S(1)}, u32[]{:S(2)}, u32[]{:S(2)}) collective-permute-start(f32[3,7,256]{2,1,0:T(8,128)S(1)} %copy-done.5), channel_id=1, source_target_pairs={{0,8},{4,12},{8,0},{12,4},{16,24},{20,28},{24,16},{28,20},{1,9},{5... | collective-permute-start | bytes 64520 | tf_op jit(solution)/shard_map/ppermute | solution.py:242
  132.7 3.8 %copy-start.7 = (f32[3,7,256]{2,1,0:T(8,128)}, f32[3,7,256]{2,1,0:T(8,128)S(1)}, u32[]{:S(2)}) copy-start(f32[3,7,256]{2,1,0:T(8,128)S(1)} %collective-permute-done.5.refs_6_) | copy-start | bytes 64516
  132.7 3.8 %collective-permute-start = (f32[3,7,256]{2,1,0:T(8,128)S(1)}, f32[3,7,256]{2,1,0:T(8,128)S(1)}, u32[]{:S(2)}, u32[]{:S(2)}) collective-permute-start(f32[3,7,256]{2,1,0:T(8,128)S(1)} %copy-done.5), channel_id=1, source_target_pairs={{0,4},{4,0},{8,12},{12,8},{16,20},{20,16},{24,28},{28,24},{1,5},{5... | collective-permute-start | bytes 64520 | tf_op jit(solution)/shard_map/ppermute | solution.py:242
  133.4 3.0 %copy-start.8 = (f32[3,7,256]{2,1,0:T(8,128)}, f32[3,7,256]{2,1,0:T(8,128)S(1)}, u32[]{:S(2)}) copy-start(f32[3,7,256]{2,1,0:T(8,128)S(1)} %collective-permute-done.4.refs_5_) | copy-start | bytes 64516
  133.4 3.0 %copy-start.9 = (f32[3,7,256]{2,1,0:T(8,128)}, f32[3,7,256]{2,1,0:T(8,128)S(1)}, u32[]{:S(2)}) copy-start(f32[3,7,256]{2,1,0:T(8,128)S(1)} %collective-permute-done.3.refs_4_) | copy-start | bytes 64516
  133.5 3.0 %copy-start.10 = (f32[3,7,256]{2,1,0:T(8,128)}, f32[3,7,256]{2,1,0:T(8,128)S(1)}, u32[]{:S(2)}) copy-start(f32[3,7,256]{2,1,0:T(8,128)S(1)} %collective-permute-done.2.refs_3_) | copy-start | bytes 64516
  134.5 2.1 %copy-start.11 = (f32[3,7,256]{2,1,0:T(8,128)}, f32[3,7,256]{2,1,0:T(8,128)S(1)}, u32[]{:S(2)}) copy-start(f32[3,7,256]{2,1,0:T(8,128)S(1)} %collective-permute-done.1.refs_2_) | copy-start | bytes 64516
  136.5 0.6 copy-start.12
  140.5 1.2 copy-start.1

commit v4 on v3

--- a/solution.py
+++ b/solution.py
@@ -18,11 +18,15 @@
     return lax.dot_general(a, b, (dims, ((), ())), preferred_element_type=jnp.float32)
 
 
+def room(mebibytes):
+    return pltpu.CompilerParams(vmem_limit_bytes=mebibytes << 20)
+
+
 def estimate(flops, moved):
     return pl.CostEstimate(flops=flops, bytes_accessed=moved, transcendentals=0)
 
 
-def split_columns(x, members, tp):
+def split_columns(x, members, tp, mebibytes):
     streams, rows, channels = x.shape
     width = channels // tp // members
     steps = 2 if tp % 2 == 0 else 1
@@ -41,6 +45,7 @@
         out_specs=pl.BlockSpec((members, part, streams, rows, width), lambda i: (0, i, 0, 0, 0)),
         out_shape=jax.ShapeDtypeStruct((members, tp, streams, rows, width), x.dtype),
         cost_estimate=estimate(0, 4 * x.size),
+        compiler_params=room(mebibytes),
         name="split_columns",
     )(x)
 
@@ -54,15 +59,16 @@
         for t in range(part):
             for c in range(members):
                 at = (t * members + c) * width
-                o_ref[:, :, at : at + width] = x_ref[c, t]
+                o_ref[:, :, at : at + width] = x_ref[c, pl.program_id(0) * part + t]
 
     return pl.pallas_call(
         kernel,
         grid=(steps,),
-        in_specs=[pl.BlockSpec((members, part, streams, rows, width), lambda i: (0, i, 0, 0, 0))],
+        in_specs=[pl.BlockSpec(memory_space=pltpu.VMEM)],
         out_specs=pl.BlockSpec((streams, rows, part * members * width), lambda i: (0, 0, i)),
         out_shape=jax.ShapeDtypeStruct((streams, rows, tp * members * width), x.dtype),
         cost_estimate=estimate(0, 4 * x.size),
+        compiler_params=room(10),
         name="join_columns",
     )(x)
 
@@ -137,6 +143,7 @@
             jax.ShapeDtypeStruct((members, tokens // members, width), jnp.bfloat16),
         ],
         cost_estimate=estimate(10_000_000_000, 8 * x.size),
+        compiler_params=room(16),
         name="forward",
     )(docs, x, taps)
 
@@ -223,6 +230,7 @@
             jax.ShapeDtypeStruct(taps.shape, jnp.float32),
         ],
         cost_estimate=estimate(20_000_000_000, 12 * x.size),
+        compiler_params=room(24),
         name="backward",
     )(docs, x, taps, mixed, att, up)
 
@@ -234,51 +242,60 @@
     ).reshape(shape)
 
 
-def gather_columns(piece, members):
+def gather_columns(piece, members, after):
     count = lax.axis_size("ctx")
+    position = lax.axis_index("ctx").astype(jnp.int32)
     streams, taps, width = piece.shape
-    pieces = [piece]
-    for step in range(1, count):
-        pieces.append(lax.ppermute(piece, "ctx", [(i, i ^ step) for i in range(count)]))
-    position = lax.axis_index("ctx").astype(jnp.int32).reshape(1)
+    other = lax.ppermute(piece, "ctx", [(i, i ^ 1) for i in range(count)])
+    even = position % 2 == 0
+    pair = jnp.concatenate(
+        [jnp.where(even, piece, other), jnp.where(even, other, piece)], axis=-1
+    )
+    pair, after = lax.optimization_barrier((pair, after))
+    pairs = [pair]
+    for step in range(2, count, 2):
+        pairs.append(lax.ppermute(pair, "ctx", [(i, i ^ step) for i in range(count)]))
 
     def kernel(position_ref, *refs):
         o_ref = refs[-1]
-        for step in range(members):
-            column = lax.rem(position_ref[0] ^ step, members)
-            at = pl.multiple_of(column * width, width)
-            total = refs[step][...]
-            for other in range(step + members, count, members):
-                total = total + refs[other][...]
-            o_ref[:, :, pl.ds(at, width)] = total
-
-    whole = pl.BlockSpec((streams, taps, width), lambda i, p: (0, 0, 0))
-    return pl.pallas_call(
+        for step in range(0, members, 2):
+            column = lax.rem(position_ref[0] ^ step, members) // 2
+            at = pl.multiple_of(column * 2 * width, 2 * width)
+            total = refs[step // 2][...]
+            for further in range(step + members, count, members):
+                total = total + refs[further // 2][...]
+            o_ref[:, :, pl.ds(at, 2 * width)] = total
+
+    whole = pl.BlockSpec((streams, taps, 2 * width), lambda i, p: (0, 0, 0))
+    gathered = pl.pallas_call(
         kernel,
         grid_spec=pltpu.PrefetchScalarGridSpec(
             num_scalar_prefetch=1,
             grid=(1,),
-            in_specs=[whole] * count,
+            in_specs=[whole] * (count // 2),
             out_specs=pl.BlockSpec((streams, taps, members * width), lambda i, p: (0, 0, 0)),
         ),
         out_shape=jax.ShapeDtypeStruct((streams, taps, members * width), piece.dtype),
+        compiler_params=room(4),
         name="place_columns",
-    )(position, *pieces)
+    )(position.reshape(1), *pairs)
+    return gathered, after
 
 
 def by_heads(qkv, filters, doc_ids, upstream):
     members, tp = lax.axis_size("ctx"), lax.axis_size("tp")
     width = upstream.shape[1] // members
     position = lax.axis_index("ctx")
-    slabs = split_columns(jnp.transpose(qkv, (1, 0, 2)), members, tp)
+    slabs = split_columns(jnp.transpose(qkv, (1, 0, 2)), members, tp, 60)
     x = swap(slabs.reshape((members * tp,) + slabs.shape[2:]), AXES)
-    up = swap(split_columns(upstream[None], members, 1)[:, 0, 0], "ctx")
+    up = swap(split_columns(upstream[None], members, 1, 10)[:, 0, 0], "ctx")
     taps = lax.dynamic_slice_in_dim(filters, position * width, width, 2)
     mixed, att = forward(doc_ids, x, taps, members)
     attended = join_columns(swap(att, "ctx")[:, None, None])[0]
     grad, tap_grad = backward(doc_ids, x, taps, mixed, att, up)
     qkv_grad = join_columns(swap(grad, AXES).reshape(slabs.shape))
-    return attended, jnp.transpose(qkv_grad, (1, 0, 2)), gather_columns(tap_grad, members)
+    filter_grad, attended = gather_columns(tap_grad, members, attended)
+    return attended, jnp.transpose(qkv_grad, (1, 0, 2)), filter_grad
 
 
 def from_behind(value, axis, steps):

time: 145 us -> 135 us (0.931)
  starting transfers between devices: 40.4 us -> 28.5 us
  waiting for transfers between devices: 68.3 us -> 76.3 us
  Pallas kernels: 31.4 us -> 25.1 us
    ppermute x7 -> x4, starting transfers between devices: 20.7 us -> 7.7 us  [the longest x3 5.87 us: gather_columns(): lax.ppermute(pair, 'ctx', [(i, i ^ step) for i in range(count)])]
    ppermute x7 -> x4, waiting for transfers between devices: 25.2 us -> 32.8 us  [the longest x3 25.7 us: gather_columns(): lax.ppermute(pair, 'ctx', [(i, i ^ step) for i in range(count)])]
    pallas_call x2, Pallas kernels: 4.23 us -> 2.06 us  [join_columns(): pl.pallas_call(kernel, grid=(steps,), in_specs=[pl.BlockSpec(memory_space...]
    unnamed x26 -> x12, local copies, waits for them, and re-layouts: 2.59 us -> 3.7 us
  transfers between devices with their start and end apart: 11 -> 8, of which waited for: 6 -> 5; matrix products, arithmetic and copies ran while one was open for 0% -> 0% of each run, Pallas kernels for 19% -> 16%
where the time goes in v4:
time: 135 us; the launch traced here: 134 us
  waiting for transfers between devices  76.3 us (57%)
  starting transfers between devices  28.5 us (21%)
  Pallas kernels  25.1 us (19%)
  local copies, waits for them, and re-layouts  3.71 us (3%)
    all_to_all x4, waiting for transfers between devices, swap(): lax.all_to_all(value.reshape(shape[0], -1, shape[-1]), axes, split_axis=0...  43.5 us
    ppermute x3, waiting for transfers between devices, gather_columns(): lax.ppermute(pair, 'ctx', [(i, i ^ step) for i in range(count)])  25.7 us
    all_to_all x4, starting transfers between devices, swap(): lax.all_to_all(value.reshape(shape[0], -1, shape[-1]), axes, split_axis=0...  20.8 us
    pallas_call x1, Pallas kernels, backward(): pl.pallas_call(backward_kernel, grid_spec=pltpu.PrefetchScalarGridSpec(nu...  12.3 us
    ppermute x1, waiting for transfers between devices, gather_columns(): other = lax.ppermute(piece, 'ctx', [(i, i ^ 1) for i in range(count)])  7.06 us
    pallas_call x1, Pallas kernels, forward(): pl.pallas_call(forward_kernel, grid_spec=pltpu.PrefetchScalarGridSpec(num...  6.79 us
    ppermute x3, starting transfers between devices, gather_columns(): lax.ppermute(pair, 'ctx', [(i, i ^ step) for i in range(count)])  5.87 us
    unnamed x12, local copies, waits for them, and re-layouts  3.7 us
  transfers between devices with their start and end apart: 8, of which 5 were waited for; matrix products, arithmetic and copies ran while one was open for 0% of the time, Pallas kernels for 16%

profile of v4, /device:TPU:0, one launch (start us, length us, event | category | flops | bytes accessed | tf_op | source)
XLA Modules:
  0.0 134.4 jit_solution(9795358128781579544)
XLA Ops:
  0.6 0.0 copy-start
  0.6 2.4 %split_columns.2 = bf16[8,4,3,32,256]{4,3,2,1,0:T(8,128)(2,1)} custom-call(bf16[3,32,8192]{2,1,0:T(8,128)(2,1)} %bitcast.18), custom_call_target="tpu_custom_call" | custom-call | bytes 3145728 | tf_op jit(solution)/shard_map/split_columns/pallas_call | solution.py:41
  3.0 0.0 copy-start.2
  3.0 7.3 %all-to-all-start = ((bf16[32,96,256]{2,1,0:T(8,128)(2,1)}), bf16[32,96,256]{2,1,0:T(8,128)(2,1)S(1)}, u32[]{:S(2)}, u32[]{:S(2)}) async-start(bf16[32,96,256]{2,1,0:T(8,128)(2,1)} %bitcast.17), calls=%async_computation | async-start | bytes 3145728 | tf_op jit(solution)/shard_map/all_to_all | solution.py:240
  10.3 0.0 copy-start.3
  10.3 0.0 copy-done.2
  10.3 0.8 split_columns.3
  11.2 0.0 copy-done
  11.2 36.9 %all-to-all-done = bf16[32,96,256]{2,1,0:T(8,128)(2,1)S(1)} async-done(((bf16[32,96,256]{2,1,0:T(8,128)(2,1)}), bf16[32,96,256]{2,1,0:T(8,128)(2,1)S(1)}, u32[]{:S(2)}, u32[]{:S(2)}) %all-to-all-start) | async-done | bytes 1572896 | tf_op jit(solution)/shard_map/all_to_all | solution.py:240
  48.1 3.5 %all-to-all-start.1 = ((bf16[8,128,256]{2,1,0:T(8,128)(2,1)}), bf16[8,128,256]{2,1,0:T(8,128)(2,1)S(1)}, u32[]{:S(2)}, u32[]{:S(2)}) async-start(bf16[8,128,256]{2,1,0:T(8,128)(2,1)} %bitcast.4), calls=%async_computation.1 | async-start | bytes 1048576 | tf_op jit(solution)/shard_map/all_to_all | solution.py:240
  51.6 0.0 copy-done.3
  51.6 6.8 %forward.1 = (bf16[2,3,1024,128]{3,2,1,0:T(8,128)(2,1)S(1)}, bf16[8,128,256]{2,1,0:T(8,128)(2,1)}) custom-call(s32[8]{0:T(128)S(1)} %copy-done.3, bf16[32,3,32,256]{3,2,1,0:T(8,128)(2,1)S(1)} %bitcast.14, f32[3,7,256]{2,1,0:T(8,128)S(1)} %constant_dynamic-slice_fusion.taps_ref), custom_call_target="tpu_custom_call" | custom-call | flops 10000000000 | bytes 6291456 | tf_op jit(solution)/shard_map/forward/pallas_call | solution.py:126
  58.4 0.0 copy-start.4
  58.4 1.1 copy-done.4
  59.5 6.7 %all-to-all-done.1.up_ref = bf16[8,128,256]{2,1,0:T(8,128)(2,1)S(1)} async-done(((bf16[8,128,256]{2,1,0:T(8,128)(2,1)}), bf16[8,128,256]{2,1,0:T(8,128)(2,1)S(1)}, u32[]{:S(2)}, u32[]{:S(2)}) %all-to-all-start.1) | async-done | bytes 524320 | tf_op jit(solution)/shard_map/all_to_all | solution.py:240
  66.2 3.6 %all-to-all-start.2 = ((bf16[8,128,256]{2,1,0:T(8,128)(2,1)}), bf16[8,128,256]{2,1,0:T(8,128)(2,1)S(1)}, u32[]{:S(2)}, u32[]{:S(2)}) async-start(bf16[8,128,256]{2,1,0:T(8,128)(2,1)} %get-tuple-element.10.att_ref), calls=%async_computation.2 | async-start | bytes 1048576 | tf_op jit(solution)/shard_map/all_to_all | solution.py:240
  69.8 0.0 copy-start.5
  69.8 1.4 %copy-done.5 = bf16[2,3,1024,128]{3,2,1,0:T(8,128)(2,1)S(1)} copy-done((bf16[2,3,1024,128]{3,2,1,0:T(8,128)(2,1)S(1)}, bf16[2,3,1024,128]{3,2,1,0:T(8,128)(2,1)}, u32[]{:S(2)}) %copy-start.5) | copy-done | bytes 1572888
  71.2 12.3 %backward.1 = (bf16[32,3,32,256]{3,2,1,0:T(8,128)(2,1)S(1)}, f32[3,7,256]{2,1,0:T(8,128)S(1)}) custom-call(s32[8]{0:T(128)S(1)} %copy-done.3, bf16[32,3,32,256]{3,2,1,0:T(8,128)(2,1)S(1)} %bitcast.15, f32[3,7,256]{2,1,0:T(8,128)S(1)} %constant_dynamic-slice_fusion.taps_ref, bf16[2,3,1024,128]{3,2,1,0:T(8,128)(2,1)S(1)} %copy-done.5, ...), custom_call_target="tpu_custom_call" | custom-call | flops 20000000000 | bytes 9437184 | tf_op jit(solution)/shard_map/backward/pallas_call | solution.py:210
  83.6 0.0 copy-start.1
  83.6 1.1 copy-done.1
  84.7 0.0 all-to-all-done.2
  84.7 6.4 %all-to-all-start.3 = ((bf16[32,96,256]{2,1,0:T(8,128)(2,1)}), bf16[32,96,256]{2,1,0:T(8,128)(2,1)S(1)}, u32[]{:S(2)}, u32[]{:S(2)}) async-start(bf16[32,96,256]{2,1,0:T(8,128)(2,1)} %bitcast.13), calls=%async_computation.3 | async-start | bytes 3145728 | tf_op jit(solution)/shard_map/all_to_all | solution.py:240
  91.1 1.8 %collective-permute-start = (f32[3,7,256]{2,1,0:T(8,128)S(1)}, f32[3,7,256]{2,1,0:T(8,128)S(1)}, u32[]{:S(2)}, u32[]{:S(2)}) collective-permute-start(f32[3,7,256]{2,1,0:T(8,128)S(1)} %get-tuple-element.11), channel_id=1, source_target_pairs={{0,4},{4,0},{8,12},{12,8},{16,20},{20,16},{24,28},{28,24},{1,5},{5... | collective-permute-start | bytes 64520 | tf_op jit(solution)/shard_map/ppermute | solution.py:249
  92.9 7.1 %collective-permute-done = f32[3,7,256]{2,1,0:T(8,128)S(1)} collective-permute-done((f32[3,7,256]{2,1,0:T(8,128)S(1)}, f32[3,7,256]{2,1,0:T(8,128)S(1)}, u32[]{:S(2)}, u32[]{:S(2)}) %collective-permute-start) | collective-permute-done | bytes 21536 | tf_op jit(solution)/shard_map/ppermute | solution.py:249
  100.0 0.8 join_columns.2
  100.8 0.8 collective-permute-start.1
  101.7 5.0 %collective-permute-start.2 = (f32[3,7,512]{2,1,0:T(8,128)S(1)}, f32[3,7,512]{2,1,0:T(8,128)S(1)}, u32[]{:S(2)}, u32[]{:S(2)}) collective-permute-start(f32[3,7,512]{2,1,0:T(8,128)S(1)} %pad_maximum_fusion.refs_0_), channel_id=1, source_target_pairs={{0,16},{4,20},{8,24},{12,28},{16,0},{20,4},{24,8},{28,12},{1,17},{... | collective-permute-start | bytes 129032 | tf_op jit(solution)/shard_map/ppermute | solution.py:257
  106.7 0.0 collective-permute-start.3
  106.7 12.1 %collective-permute-done.1.refs_1_ = f32[3,7,512]{2,1,0:T(8,128)S(1)} collective-permute-done((f32[3,7,512]{2,1,0:T(8,128)S(1)}, f32[3,7,512]{2,1,0:T(8,128)S(1)}, u32[]{:S(2)}, u32[]{:S(2)}) %collective-permute-start.1) | collective-permute-done | bytes 43040 | tf_op jit(solution)/shard_map/ppermute | solution.py:257
  118.8 13.6 %collective-permute-done.2.refs_2_ = f32[3,7,512]{2,1,0:T(8,128)S(1)} collective-permute-done((f32[3,7,512]{2,1,0:T(8,128)S(1)}, f32[3,7,512]{2,1,0:T(8,128)S(1)}, u32[]{:S(2)}, u32[]{:S(2)}) %collective-permute-start.2) | collective-permute-done | bytes 43040 | tf_op jit(solution)/shard_map/ppermute | solution.py:257
  132.4 0.0 collective-permute-done.3.refs_3_
  132.5 0.7 place_columns.1
  133.2 0.0 all-to-all-done.3
  133.2 1.2 join_columns.3
  (3 shorter events, 0.0 us)
Async XLA Ops:
  0.6 10.6 %copy-start = (f32[3,7,2048]{2,1,0:T(8,128)S(1)}, f32[3,7,2048]{2,1,0:T(8,128)}, u32[]{:S(2)}) copy-start(f32[3,7,2048]{2,1,0:T(8,128)} %param.5) | copy-start | bytes 516100
  3.0 7.3 %copy-start.2 = (bf16[128,2048]{1,0:T(8,128)(2,1)S(1)}, bf16[128,2048]{1,0:T(8,128)(2,1)}, u32[]{:S(2)}) copy-start(bf16[128,2048]{1,0:T(8,128)(2,1)} %param.7) | copy-start | bytes 1572868
  3.0 45.0 %all-to-all-start = ((bf16[32,96,256]{2,1,0:T(8,128)(2,1)}), bf16[32,96,256]{2,1,0:T(8,128)(2,1)S(1)}, u32[]{:S(2)}, u32[]{:S(2)}) async-start(bf16[32,96,256]{2,1,0:T(8,128)(2,1)} %bitcast.17), calls=%async_computation | async-start | bytes 3145728 | tf_op jit(solution)/shard_map/all_to_all | solution.py:240
  10.3 41.2 %copy-start.3 = (s32[8]{0:T(128)S(1)}, s32[8]{0:T(128)}, u32[]{:S(2)}) copy-start(s32[8]{0:T(128)} %docs.3) | copy-start | bytes 100
  48.1 18.1 %all-to-all-start.1 = ((bf16[8,128,256]{2,1,0:T(8,128)(2,1)}), bf16[8,128,256]{2,1,0:T(8,128)(2,1)S(1)}, u32[]{:S(2)}, u32[]{:S(2)}) async-start(bf16[8,128,256]{2,1,0:T(8,128)(2,1)} %bitcast.4), calls=%async_computation.1 | async-start | bytes 1048576 | tf_op jit(solution)/shard_map/all_to_all | solution.py:240
  58.4 1.1 copy-start.4
  66.2 18.5 %all-to-all-start.2 = ((bf16[8,128,256]{2,1,0:T(8,128)(2,1)}), bf16[8,128,256]{2,1,0:T(8,128)(2,1)S(1)}, u32[]{:S(2)}, u32[]{:S(2)}) async-start(bf16[8,128,256]{2,1,0:T(8,128)(2,1)} %get-tuple-element.10.att_ref), calls=%async_computation.2 | async-start | bytes 1048576 | tf_op jit(solution)/shard_map/all_to_all | solution.py:240
  69.8 1.4 %copy-start.5 = (bf16[2,3,1024,128]{3,2,1,0:T(8,128)(2,1)S(1)}, bf16[2,3,1024,128]{3,2,1,0:T(8,128)(2,1)}, u32[]{:S(2)}) copy-start(bf16[2,3,1024,128]{3,2,1,0:T(8,128)(2,1)} %copy-done.4) | copy-start | bytes 4718596
  83.6 1.1 copy-start.1
  84.7 48.5 %all-to-all-start.3 = ((bf16[32,96,256]{2,1,0:T(8,128)(2,1)}), bf16[32,96,256]{2,1,0:T(8,128)(2,1)S(1)}, u32[]{:S(2)}, u32[]{:S(2)}) async-start(bf16[32,96,256]{2,1,0:T(8,128)(2,1)} %bitcast.13), calls=%async_computation.3 | async-start | bytes 3145728 | tf_op jit(solution)/shard_map/all_to_all | solution.py:240
  91.1 8.9 %collective-permute-start = (f32[3,7,256]{2,1,0:T(8,128)S(1)}, f32[3,7,256]{2,1,0:T(8,128)S(1)}, u32[]{:S(2)}, u32[]{:S(2)}) collective-permute-start(f32[3,7,256]{2,1,0:T(8,128)S(1)} %get-tuple-element.11), channel_id=1, source_target_pairs={{0,4},{4,0},{8,12},{12,8},{16,20},{20,16},{24,28},{28,24},{1,5},{5... | collective-permute-start | bytes 64520 | tf_op jit(solution)/shard_map/ppermute | solution.py:249
  100.8 18.0 %collective-permute-start.1 = (f32[3,7,512]{2,1,0:T(8,128)S(1)}, f32[3,7,512]{2,1,0:T(8,128)S(1)}, u32[]{:S(2)}, u32[]{:S(2)}) collective-permute-start(f32[3,7,512]{2,1,0:T(8,128)S(1)} %pad_maximum_fusion.refs_0_), channel_id=1, source_target_pairs={{0,8},{4,12},{8,0},{12,4},{16,24},{20,28},{24,16},{28,20},{1,9},{5... | collective-permute-start | bytes 129032 | tf_op jit(solution)/shard_map/ppermute | solution.py:257
  101.7 30.8 %collective-permute-start.2 = (f32[3,7,512]{2,1,0:T(8,128)S(1)}, f32[3,7,512]{2,1,0:T(8,128)S(1)}, u32[]{:S(2)}, u32[]{:S(2)}) collective-permute-start(f32[3,7,512]{2,1,0:T(8,128)S(1)} %pad_maximum_fusion.refs_0_), channel_id=1, source_target_pairs={{0,16},{4,20},{8,24},{12,28},{16,0},{20,4},{24,8},{28,12},{1,17},{... | collective-permute-start | bytes 129032 | tf_op jit(solution)/shard_map/ppermute | solution.py:257
  106.7 25.7 %collective-permute-start.3 = (f32[3,7,512]{2,1,0:T(8,128)S(1)}, f32[3,7,512]{2,1,0:T(8,128)S(1)}, u32[]{:S(2)}, u32[]{:S(2)}) collective-permute-start(f32[3,7,512]{2,1,0:T(8,128)S(1)} %pad_maximum_fusion.refs_0_), channel_id=1, source_target_pairs={{0,24},{4,28},{8,16},{12,20},{16,8},{20,12},{24,0},{28,4},{1,25},{... | collective-permute-start | bytes 129032 | tf_op jit(solution)/shard_map/ppermute | solution.py:257

commit v5 on v4

--- a/solution.py
+++ b/solution.py
@@ -1,3 +1,5 @@
+import functools
+
 import jax
 import jax.numpy as jnp
 from jax import lax
@@ -91,10 +93,10 @@
     return expo, jnp.sum(expo, axis=1, keepdims=True)
 
 
-def forward_kernel(docs, x_ref, taps_ref, mixed_ref, out_ref, padded):
+def forward_kernel(docs, x_ref, taps_ref, before_ref, mixed_ref, out_ref, padded):
     sources, streams, rows, _ = x_ref.shape
     tokens = sources * rows
-    padded[:, 0:PAD, :] = jnp.zeros((streams, PAD, HEAD_DIM), jnp.float32)
+    padded[:, 0:PAD, :] = before_ref[...].astype(jnp.float32)
     for m in range(streams):
         padded[m, PAD:, :] = x_ref[:, m].reshape(tokens, HEAD_DIM).astype(jnp.float32)
     for m in range(streams):
@@ -119,7 +121,7 @@
         )
 
 
-def forward(docs, x, taps, members):
+def forward(docs, x, taps, before, members):
     sources, streams, rows, width = x.shape
     per = width // HEAD_DIM
     tokens = sources * rows
@@ -131,6 +133,7 @@
             in_specs=[
                 pl.BlockSpec((sources, streams, rows, HEAD_DIM), lambda h, d: (0, 0, 0, h)),
                 pl.BlockSpec((streams, KW, HEAD_DIM), lambda h, d: (0, 0, h)),
+                pl.BlockSpec((streams, PAD, HEAD_DIM), lambda h, d: (0, 0, h)),
             ],
             out_specs=[
                 pl.BlockSpec((1, streams, tokens, HEAD_DIM), lambda h, d: (h, 0, 0, 0)),
@@ -145,11 +148,23 @@
         cost_estimate=estimate(10_000_000_000, 8 * x.size),
         compiler_params=room(16),
         name="forward",
-    )(docs, x, taps)
+    )(docs, x, taps, before)
 
 
 def backward_kernel(
-    docs, x_ref, taps_ref, mixed_ref, att_ref, up_ref, grad_ref, tapg_ref, padded, cgrad
+    docs,
+    x_ref,
+    taps_ref,
+    before_ref,
+    mixed_ref,
+    att_ref,
+    up_ref,
+    grad_ref,
+    tapg_ref,
+    head_ref,
+    tail_ref,
+    padded,
+    cgrad,
 ):
     sources, streams, rows, _ = x_ref.shape
     tokens = sources * rows
@@ -175,7 +190,8 @@
         cgrad[0, own, :] = dot(dscore, keys, ((1,), (0,)))
         cgrad[1, span, :] += dot(dscore, query, ((0,), (0,)))
         cgrad[2, span, :] += dot(prob.astype(jnp.bfloat16), up, ((0,), (0,)))
-    padded[:, 0:PAD, :] = jnp.zeros((streams, PAD, HEAD_DIM), jnp.float32)
+    padded[:, 0:PAD, :] = before_ref[...].astype(jnp.float32)
+    head_ref[...] = cgrad[:, 0:PAD, :]
     for m in range(streams):
         padded[m, PAD:, :] = x_ref[:, m].reshape(tokens, HEAD_DIM).astype(jnp.float32)
     for m in range(streams):
@@ -195,17 +211,19 @@
             grad_ref[start // rows : (start + BLOCK) // rows, m] = total.astype(
                 jnp.bfloat16
             ).reshape(BLOCK // rows, rows, HEAD_DIM)
+        tail_ref[m] = total[BLOCK - PAD :]
         for lag in range(KW):
             tapg_ref[m, lag : lag + 1, :] = jnp.sum(sums[lag], axis=0, keepdims=True)
 
 
-def backward(docs, x, taps, mixed, att, up):
+def backward(docs, x, taps, before, mixed, att, up):
     sources, streams, rows, width = x.shape
     per = width // HEAD_DIM
     tokens = sources * rows
     members = att.shape[0]
     slab = pl.BlockSpec((sources, streams, rows, HEAD_DIM), lambda h, d: (0, 0, 0, h))
     tap = pl.BlockSpec((streams, KW, HEAD_DIM), lambda h, d: (0, 0, h))
+    edge = pl.BlockSpec((streams, PAD, HEAD_DIM), lambda h, d: (0, 0, h))
     rowspec = pl.BlockSpec((members, tokens // members, HEAD_DIM), lambda h, d: (0, 0, h))
     return pl.pallas_call(
         backward_kernel,
@@ -215,11 +233,12 @@
             in_specs=[
                 slab,
                 tap,
+                edge,
                 pl.BlockSpec((1, streams, tokens, HEAD_DIM), lambda h, d: (h, 0, 0, 0)),
                 rowspec,
                 rowspec,
             ],
-            out_specs=[slab, tap],
+            out_specs=[slab, tap, edge, edge],
             scratch_shapes=[
                 pltpu.VMEM((streams, tokens + PAD, HEAD_DIM), jnp.float32),
                 pltpu.VMEM((streams, tokens + PAD, HEAD_DIM), jnp.float32),
@@ -228,73 +247,103 @@
         out_shape=[
             jax.ShapeDtypeStruct(x.shape, jnp.bfloat16),
             jax.ShapeDtypeStruct(taps.shape, jnp.float32),
+            jax.ShapeDtypeStruct((streams, PAD, width), jnp.float32),
+            jax.ShapeDtypeStruct((streams, PAD, width), jnp.float32),
         ],
         cost_estimate=estimate(20_000_000_000, 12 * x.size),
         compiler_params=room(24),
         name="backward",
-    )(docs, x, taps, mixed, att, up)
-
-
-def swap(value, axes):
+    )(docs, x, taps, before, mixed, att, up)
+
+
+def swap(value, axes, groups):
     shape = value.shape
     return lax.all_to_all(
-        value.reshape(shape[0], -1, shape[-1]), axes, split_axis=0, concat_axis=0, tiled=True
+        value.reshape(shape[0], -1, shape[-1]),
+        axes,
+        split_axis=0,
+        concat_axis=0,
+        axis_index_groups=groups,
+        tiled=True,
     ).reshape(shape)
+
+
+def across(value, step):
+    count = lax.axis_size("ctx")
+    return lax.ppermute(value, "ctx", [(i, i ^ step) for i in range(count)])
 
 
 def gather_columns(piece, members, after):
     count = lax.axis_size("ctx")
     position = lax.axis_index("ctx").astype(jnp.int32)
     streams, taps, width = piece.shape
-    other = lax.ppermute(piece, "ctx", [(i, i ^ 1) for i in range(count)])
-    even = position % 2 == 0
-    pair = jnp.concatenate(
-        [jnp.where(even, piece, other), jnp.where(even, other, piece)], axis=-1
-    )
-    pair, after = lax.optimization_barrier((pair, after))
-    pairs = [pair]
-    for step in range(2, count, 2):
-        pairs.append(lax.ppermute(pair, "ctx", [(i, i ^ step) for i in range(count)]))
+    if members < count:
+        span, held = 1, piece + across(piece, members)
+    else:
+        span, other = 2, across(piece, 1)
+        even = position % 2 == 0
+        held = jnp.concatenate(
+            [jnp.where(even, piece, other), jnp.where(even, other, piece)], axis=-1
+        )
+    held, after = lax.optimization_barrier((held, after))
+    steps = range(0, members, span)
+    pieces = [across(held, step) if step else held for step in steps]
 
     def kernel(position_ref, *refs):
         o_ref = refs[-1]
-        for step in range(0, members, 2):
-            column = lax.rem(position_ref[0] ^ step, members) // 2
-            at = pl.multiple_of(column * 2 * width, 2 * width)
-            total = refs[step // 2][...]
-            for further in range(step + members, count, members):
-                total = total + refs[further // 2][...]
-            o_ref[:, :, pl.ds(at, 2 * width)] = total
-
-    whole = pl.BlockSpec((streams, taps, 2 * width), lambda i, p: (0, 0, 0))
+        for step in steps:
+            column = lax.rem(position_ref[0] ^ step, members) // span
+            at = pl.multiple_of(column * span * width, span * width)
+            o_ref[:, :, pl.ds(at, span * width)] = refs[step // span][...]
+
     gathered = pl.pallas_call(
         kernel,
         grid_spec=pltpu.PrefetchScalarGridSpec(
             num_scalar_prefetch=1,
             grid=(1,),
-            in_specs=[whole] * (count // 2),
+            in_specs=[pl.BlockSpec((streams, taps, span * width), lambda i, p: (0, 0, 0))]
+            * len(pieces),
             out_specs=pl.BlockSpec((streams, taps, members * width), lambda i, p: (0, 0, 0)),
         ),
         out_shape=jax.ShapeDtypeStruct((streams, taps, members * width), piece.dtype),
         compiler_params=room(4),
         name="place_columns",
-    )(position.reshape(1), *pairs)
+    )(position.reshape(1), *pieces)
     return gathered, after
 
 
-def by_heads(qkv, filters, doc_ids, upstream):
-    members, tp = lax.axis_size("ctx"), lax.axis_size("tp")
+def by_heads(parts, qkv, filters, doc_ids, upstream):
+    count, tp = lax.axis_size("ctx"), lax.axis_size("tp")
+    members = count // parts
+    rows, streams, _ = qkv.shape
     width = upstream.shape[1] // members
     position = lax.axis_index("ctx")
+    every = everywhere = None
+    if parts > 1:
+        every = [[p * members + c for c in range(members)] for p in range(parts)]
+        everywhere = [[c * tp + t for c in group for t in range(tp)] for group in every]
+        blocks = doc_ids.shape[0] // parts
+        doc_ids = lax.dynamic_slice_in_dim(doc_ids, position // members * blocks, blocks)
     slabs = split_columns(jnp.transpose(qkv, (1, 0, 2)), members, tp, 60)
-    x = swap(slabs.reshape((members * tp,) + slabs.shape[2:]), AXES)
-    up = swap(split_columns(upstream[None], members, 1, 10)[:, 0, 0], "ctx")
-    taps = lax.dynamic_slice_in_dim(filters, position * width, width, 2)
-    mixed, att = forward(doc_ids, x, taps, members)
-    attended = join_columns(swap(att, "ctx")[:, None, None])[0]
-    grad, tap_grad = backward(doc_ids, x, taps, mixed, att, up)
-    qkv_grad = join_columns(swap(grad, AXES).reshape(slabs.shape))
+    x = swap(slabs.reshape((members * tp,) + slabs.shape[2:]), AXES, everywhere)
+    up = swap(split_columns(upstream[None], members, 1, 10)[:, 0, 0], "ctx", every)
+    taps = lax.dynamic_slice_in_dim(filters, position % members * width, width, 2)
+    if parts > 1:
+        upward = [(i, i + members) for i in range(count - members)]
+        before = lax.ppermute(x[-1, :, rows - PAD :], "ctx", upward)
+    else:
+        before = jnp.zeros((streams, PAD, width), x.dtype)
+    mixed, att = forward(doc_ids, x, taps, before, members)
+    attended = join_columns(swap(att, "ctx", every)[:, None, None])[0]
+    grad, tap_grad, head, tail = backward(doc_ids, x, taps, before, mixed, att, up)
+    if parts > 1:
+        after = lax.ppermute(head, "ctx", [(to, source) for source, to in upward])
+        after = jnp.concatenate([jnp.zeros_like(after), after], axis=1)
+        for lag in range(KW):
+            tail = tail + taps[:, lag : lag + 1] * after[:, lag : lag + PAD]
+        grad = grad.at[-1, :, rows - PAD :].set(tail.astype(grad.dtype))
     filter_grad, attended = gather_columns(tap_grad, members, attended)
+    qkv_grad = join_columns(swap(grad, AXES, everywhere).reshape(slabs.shape))
     return attended, jnp.transpose(qkv_grad, (1, 0, 2)), filter_grad
 
 
@@ -408,13 +457,20 @@
 
 
 def solution(mesh):
+    count = mesh.shape["ctx"]
+
     def shards(qkv, filters, doc_ids, upstream):
-        heads = upstream.shape[1] // HEAD_DIM
-        tokens = upstream.shape[0]
-        count = mesh.shape["ctx"]
-        whole = heads % count == 0 and tokens % BLOCK == 0 and count & (count - 1) == 0
-        form = by_heads if whole else by_ring
-        return form(qkv, filters, doc_ids, upstream)
+        tokens, width = upstream.shape
+        heads = width // HEAD_DIM
+        args = (qkv, filters, doc_ids, upstream)
+        even = tokens % BLOCK == 0 and qkv.shape[0] % PAD == 0 and count & (count - 1) == 0
+        if heads % count or not even or count < 4:
+            return by_ring(*args)
+        middle = doc_ids.shape[0] // 2
+        apart = doc_ids[middle - 1] != doc_ids[middle]
+        return lax.cond(
+            apart, functools.partial(by_heads, 2), functools.partial(by_heads, 1), *args
+        )
 
     return jax.shard_map(
         shards,

time: 135 us -> 114 us (0.84)
  waiting for transfers between devices: 76.3 us -> 51.3 us
  other arithmetic: 0.02 us -> 1.97 us
    all_to_all x4, waiting for transfers between devices: 43.5 us -> 20.6 us  [swap(): lax.all_to_all(value.reshape(shape[0], -1, shape[-1]), axes, split_axis=0...]
    unnamed x12 -> x0, local copies, waits for them, and re-layouts: 3.7 us -> none
    cond x0 -> x12, local copies, waits for them, and re-layouts: none -> 2.58 us
    ppermute x4 -> x6, starting transfers between devices: 7.7 us -> 10.2 us  [the longest x1 4.49 us: by_heads(): before = lax.ppermute(x[-1, :, rows - PAD:], 'ctx', upward)]
    all_to_all x4, starting transfers between devices: 20.8 us -> 18.3 us  [swap(): lax.all_to_all(value.reshape(shape[0], -1, shape[-1]), axes, split_axis=0...]
    ppermute x4 -> x6, waiting for transfers between devices: 32.8 us -> 30.8 us  [the longest x4 24.2 us: across(): return lax.ppermute(value, 'ctx', [(i, i ^ step) for i in range(count)])]
  transfers between devices with their start and end apart: 8 -> 10, of which waited for: 5 -> 7; matrix products, arithmetic and copies ran while one was open for 0% -> 3% of each run, Pallas kernels for 16% -> 19%
where the time goes in v5:
time: 114 us
  waiting for transfers between devices  51.3 us (45%)
  starting transfers between devices  28.5 us (25%)
  Pallas kernels  25.1 us (22%)
  local copies, waits for them, and re-layouts  4.79 us (4%)
  other arithmetic  1.97 us (2%)
  between operations  1.93 us (2%)
    ppermute x4, waiting for transfers between devices, across(): return lax.ppermute(value, 'ctx', [(i, i ^ step) for i in range(count)])  24.2 us
    all_to_all x4, waiting for transfers between devices, swap(): lax.all_to_all(value.reshape(shape[0], -1, shape[-1]), axes, split_axis=0...  20.6 us
    all_to_all x4, starting transfers between devices, swap(): lax.all_to_all(value.reshape(shape[0], -1, shape[-1]), axes, split_axis=0...  18.3 us
    pallas_call x1, Pallas kernels, backward(): pl.pallas_call(backward_kernel, grid_spec=pltpu.PrefetchScalarGridSpec(nu...  12.6 us
    pallas_call x1, Pallas kernels, forward(): pl.pallas_call(forward_kernel, grid_spec=pltpu.PrefetchScalarGridSpec(num...  6.57 us
    ppermute x1, waiting for transfers between devices, by_heads(): after = lax.ppermute(head, 'ctx', [(to, source) for source, to in upward])  5.56 us
    ppermute x1, starting transfers between devices, by_heads(): before = lax.ppermute(x[-1, :, rows - PAD:], 'ctx', upward)  4.49 us
    ppermute x4, starting transfers between devices, across(): return lax.ppermute(value, 'ctx', [(i, i ^ step) for i in range(count)])  4.44 us
  transfers between devices with their start and end apart: 10, of which 7 were waited for; matrix products, arithmetic and copies ran while one was open for 3% of the time, Pallas kernels for 19%

profile of v5, /device:TPU:0, one launch (start us, length us, event | category | flops | bytes accessed | tf_op | source)
XLA Modules:
  0.0 113.8 jit_solution(11749978433010272583)
XLA Ops:
  0.6 1.3 %fusion.13 = (s32[1]{0:T(128)}, s32[1]{0:T(128)}) fusion(s32[8]{0:T(128)} %param.10), kind=kLoop, calls=%fused_computation.40 | loop fusion | bytes 16 | tf_op jit(solution)/shard_map/slice | solution.py:470
  3.2 110.5 %conditional.1 = (bf16[128,2048]{1,0:T(8,128)(2,1)}, bf16[32,3,8192]{2,0,1:T(8,128)(2,1)}, f32[3,7,2048]{2,1,0:T(8,128)}) conditional(s32[]{:T(128)} %bitcast.24, (bf16[32,3,8192]{2,0,1:T(8,128)(2,1)}, f32[3,7,2048]{2,1,0:T(8,128)}, s32[8]{0:T(128)}, bf16[128,2048]{1,0:T(8,128)(2,1)}) %tuple.21, (s32[8]{0:T(128)}, bf16[32,3,8192]{2,0,1:T(8,128)(2,1)}, ...), branch_computations={%region_0.1_spmd, %region_1.2_spmd} | conditional | flops 30000185344 | bytes 58501976 | solution.py:471
  3.3 2.3 %split_columns.6 = bf16[4,4,3,32,512]{4,3,2,1,0:T(8,128)(2,1)} custom-call(bf16[3,32,8192]{2,1,0:T(8,128)(2,1)} %bitcast.53), custom_call_target="tpu_custom_call" | custom-call | bytes 3145728 | tf_op jit(solution)/shard_map/cond/branch_1_fun/split_columns/pallas_call | solution.py:43
  5.6 0.0 copy-start.6
  5.6 6.4 %all-to-all-start.4 = ((bf16[16,96,512]{2,1,0:T(8,128)(2,1)}), bf16[16,96,512]{2,1,0:T(8,128)(2,1)S(1)}, u32[]{:S(2)}, u32[]{:S(2)}) async-start(bf16[16,96,512]{2,1,0:T(8,128)(2,1)} %bitcast.54), calls=%async_computation.4 | async-start | bytes 3145728 | tf_op jit(solution)/shard_map/cond/branch_1_fun/all_to_all | solution.py:261
  12.0 0.0 copy-start.8
  12.1 0.0 copy-done.6
  12.1 0.8 split_columns.7
  12.9 1.3 %dynamic-slice_multiply_fusion = (f32[3,1,512]{2,1,0:T(1,128)S(1)}, f32[3,1,512]{2,1,0:T(1,128)S(1)}, f32[3,1,512]{2,1,0:T(1,128)S(1)}, f32[3,1,512]{2,1,0:T(1,1...) fusion(f32[3,7,2048]{2,1,0:T(8,128)} %get-tuple-element.40, ...), kind=kLoop, calls=%fused_computation.32 | loop fusion | flops 1536 | bytes 86044 | tf_op jit(solution)/shard_map/cond/branch_1_fun/mul | solution.py:343
  14.2 20.6 %all-to-all-done.4 = bf16[16,96,512]{2,1,0:T(8,128)(2,1)S(1)} async-done(((bf16[16,96,512]{2,1,0:T(8,128)(2,1)}), bf16[16,96,512]{2,1,0:T(8,128)(2,1)S(1)}, u32[]{:S(2)}, u32[]{:S(2)}) %all-to-all-start.4) | async-done | bytes 1572896 | tf_op jit(solution)/shard_map/cond/branch_1_fun/all_to_all | solution.py:261
  34.8 3.5 %all-to-all-start.5 = ((bf16[4,128,512]{2,1,0:T(8,128)(2,1)}), bf16[4,128,512]{2,1,0:T(8,128)(2,1)S(1)}, u32[]{:S(2)}, u32[]{:S(2)}) async-start(bf16[4,128,512]{2,1,0:T(8,128)(2,1)} %bitcast.16), calls=%async_computation.5 | async-start | bytes 1048576 | tf_op jit(solution)/shard_map/cond/branch_1_fun/all_to_all | solution.py:261
  38.3 4.5 %collective-permute-start.4 = (bf16[3,8,512]{2,1,0:T(8,128)(2,1)S(1)}, bf16[3,8,512]{2,1,0:T(8,128)(2,1)S(1)}, u32[]{:S(2)}, u32[]{:S(2)}) collective-permute-start(bf16[3,8,512]{2,1,0:T(8,128)(2,1)S(1)} %slice_bitcast_fusion), channel_id=1, source_target_pairs={{0,16},{4,20},{8,24},{12,28},{1,17},{5,21},{9,25},{13,29},{2,18},{... | collective-permute-start | bytes 73736 | tf_op jit(solution)/shard_map/cond/branch_1_fun/ppermute | solution.py:333
  42.8 0.8 constant_dynamic-slice_fusion.7.taps_ref
  43.6 0.0 copy-done.8
  43.6 0.1 dynamic_slice.7.docs
  43.7 1.0 collective-permute-done.4.before_ref
  44.6 6.6 %forward.3 = (bf16[4,3,512,128]{3,2,1,0:T(8,128)(2,1)S(1)}, bf16[4,128,512]{2,1,0:T(8,128)(2,1)}) custom-call(s32[4]{0:T(128)S(1)} %dynamic_slice.7.docs, bf16[16,3,32,512]{3,2,1,0:T(8,128)(2,1)S(1)} %bitcast.47, f32[3,7,512]{2,1,0:T(8,128)S(1)} %constant_dynamic-slice_fusion.7.taps_ref, bf16[3,8,512]{2,1,0:T(8,128)(2,1)S(1)} %collective-permute-done.4.before_ref), custom_call_target="tpu_custom_call" | custom-call | flops 10000000000 | bytes 6291456 | tf_op jit(solution)/shard_map/cond/branch_1_fun/forward/pallas_call | solution.py:128
  51.2 0.0 copy-start.1
  51.2 1.1 %copy-done.1 = bf16[4,3,512,128]{3,2,1,0:T(8,128)(2,1)} copy-done((bf16[4,3,512,128]{3,2,1,0:T(8,128)(2,1)}, bf16[4,3,512,128]{3,2,1,0:T(8,128)(2,1)S(1)}, u32[]{:S(2)}) %copy-start.1) | copy-done | bytes 1572888 | tf_op jit(solution)/shard_map/cond
  52.4 0.0 all-to-all-done.5.up_ref
  52.4 3.8 %all-to-all-start.6 = ((bf16[4,128,512]{2,1,0:T(8,128)(2,1)}), bf16[4,128,512]{2,1,0:T(8,128)(2,1)S(1)}, u32[]{:S(2)}, u32[]{:S(2)}) async-start(bf16[4,128,512]{2,1,0:T(8,128)(2,1)} %get-tuple-element.42.att_ref), calls=%async_computation.6 | async-start | bytes 1048576 | tf_op jit(solution)/shard_map/cond/branch_1_fun/all_to_all | solution.py:261
  56.1 0.0 copy-start.2
  56.1 1.4 %copy-done.2 = bf16[4,3,512,128]{3,2,1,0:T(8,128)(2,1)S(1)} copy-done((bf16[4,3,512,128]{3,2,1,0:T(8,128)(2,1)S(1)}, bf16[4,3,512,128]{3,2,1,0:T(8,128)(2,1)}, u32[]{:S(2)}) %copy-start.2) | copy-done | bytes 1572888 | tf_op jit(solution)/shard_map/cond
  57.5 12.6 %backward.3 = (bf16[16,3,32,512]{3,2,1,0:T(8,128)(2,1)}, f32[3,7,512]{2,1,0:T(8,128)S(1)}, f32[3,8,512]{2,1,0:T(8,128)S(1)}, f32[3,8,512]{2,1,0:T(8,128)S(1)}) custom-call(s32[4]{0:T(128)S(1)} %dynamic_slice.7.docs, bf16[16,3,32,512]{3,2,1,0:T(8,128)(2,1)S(1)} %bitcast.48, f32[3,7,512]{2,1,0:T(8,128)S(1)} %constant_dynamic-slice_fusion.7.taps_ref, ...), custom_call_target="tpu_custom_call" | custom-call | flops 20000000000 | bytes 9437184 | tf_op jit(solution)/shard_map/cond/branch_1_fun/backward/pallas_call | solution.py:228
  70.2 1.3 %collective-permute-start.6 = (f32[3,8,512]{2,1,0:T(8,128)S(1)}, f32[3,8,512]{2,1,0:T(8,128)S(1)}, u32[]{:S(2)}, u32[]{:S(2)}) collective-permute-start(f32[3,8,512]{2,1,0:T(8,128)S(1)} %get-tuple-element.48), channel_id=1, source_target_pairs={{16,0},{20,4},{24,8},{28,12},{17,1},{21,5},{25,9},{29,13},{18,2},{... | collective-permute-start | bytes 147464 | tf_op jit(solution)/shard_map/cond/branch_1_fun/ppermute | solution.py:340
  71.5 5.6 %collective-permute-done.6 = f32[3,8,512]{2,1,0:T(8,128)S(1)} collective-permute-done((f32[3,8,512]{2,1,0:T(8,128)S(1)}, f32[3,8,512]{2,1,0:T(8,128)S(1)}, u32[]{:S(2)}, u32[]{:S(2)}) %collective-permute-start.6) | collective-permute-done | bytes 49184 | tf_op jit(solution)/shard_map/cond/branch_1_fun/ppermute | solution.py:340
  77.0 0.7 bitcast_dynamic-update-slice_fusion
  77.7 0.0 all-to-all-done.6
  77.7 4.7 %all-to-all-start.7 = ((bf16[16,96,512]{2,1,0:T(8,128)(2,1)}), bf16[16,96,512]{2,1,0:T(8,128)(2,1)S(1)}, u32[]{:S(2)}, u32[]{:S(2)}) async-start(bf16[16,96,512]{2,1,0:T(8,128)(2,1)} %bitcast.20), calls=%async_computation.7 | async-start | bytes 3145728 | tf_op jit(solution)/shard_map/cond/branch_1_fun/all_to_all | solution.py:261
  82.4 0.1 collective-permute-start.5
  82.4 19.2 %collective-permute-done.5 = f32[3,7,512]{2,1,0:T(8,128)S(1)} collective-permute-done((f32[3,7,512]{2,1,0:T(8,128)S(1)}, f32[3,7,512]{2,1,0:T(8,128)S(1)}, u32[]{:S(2)}, u32[]{:S(2)}) %collective-permute-start.5) | collective-permute-done | bytes 43040 | tf_op jit(solution)/shard_map/cond/branch_1_fun/ppermute | solution.py:273
  101.7 0.8 join_columns.6
  102.5 2.7 %collective-permute-start.7 = (f32[3,7,512]{2,1,0:T(8,128)S(1)}, f32[3,7,512]{2,1,0:T(8,128)S(1)}, u32[]{:S(2)}, u32[]{:S(2)}) collective-permute-start(f32[3,7,512]{2,1,0:T(8,128)S(1)} %add.40.refs_0_), channel_id=1, source_target_pairs={{0,4},{4,0},{8,12},{12,8},{16,20},{20,16},{24,28},{28,24},{1,5},{5... | collective-permute-start | bytes 129032 | tf_op jit(solution)/shard_map/cond/branch_1_fun/ppermute | solution.py:273
  105.2 1.6 %collective-permute-start.8 = (f32[3,7,512]{2,1,0:T(8,128)S(1)}, f32[3,7,512]{2,1,0:T(8,128)S(1)}, u32[]{:S(2)}, u32[]{:S(2)}) collective-permute-start(f32[3,7,512]{2,1,0:T(8,128)S(1)} %add.40.refs_0_), channel_id=1, source_target_pairs={{0,8},{4,12},{8,0},{12,4},{16,24},{20,28},{24,16},{28,20},{1,9},{5... | collective-permute-start | bytes 129032 | tf_op jit(solution)/shard_map/cond/branch_1_fun/ppermute | solution.py:273
  106.9 0.0 collective-permute-start.9
  106.9 0.4 collective-permute-done.7.refs_1_
  107.3 2.0 %collective-permute-done.8.refs_2_ = f32[3,7,512]{2,1,0:T(8,128)S(1)} collective-permute-done((f32[3,7,512]{2,1,0:T(8,128)S(1)}, f32[3,7,512]{2,1,0:T(8,128)S(1)}, u32[]{:S(2)}, u32[]{:S(2)}) %collective-permute-start.8) | collective-permute-done | bytes 43040 | tf_op jit(solution)/shard_map/cond/branch_1_fun/ppermute | solution.py:273
  109.3 2.5 %collective-permute-done.9.refs_3_ = f32[3,7,512]{2,1,0:T(8,128)S(1)} collective-permute-done((f32[3,7,512]{2,1,0:T(8,128)S(1)}, f32[3,7,512]{2,1,0:T(8,128)S(1)}, u32[]{:S(2)}, u32[]{:S(2)}) %collective-permute-start.9) | collective-permute-done | bytes 43040 | tf_op jit(solution)/shard_map/cond/branch_1_fun/ppermute | solution.py:273
  111.9 0.7 place_columns.3
  112.6 0.0 all-to-all-done.7
  112.6 1.2 %join_columns.7 = bf16[3,32,8192]{2,1,0:T(8,128)(2,1)} custom-call(bf16[4,4,3,32,512]{4,3,2,1,0:T(8,128)(2,1)S(1)} %bitcast.43), custom_call_target="tpu_custom_call" | custom-call | bytes 3145728 | tf_op jit(solution)/shard_map/cond/branch_1_fun/join_columns/pallas_call | solution.py:66
  (6 shorter events, 0.0 us)
Async XLA Ops:
  5.6 6.5 %copy-start.6 = (bf16[128,2048]{1,0:T(8,128)(2,1)S(1)}, bf16[128,2048]{1,0:T(8,128)(2,1)}, u32[]{:S(2)}) copy-start(bf16[128,2048]{1,0:T(8,128)(2,1)} %get-tuple-element.43) | copy-start | bytes 1572868 | tf_op jit(solution)/shard_map/cond
  5.6 29.2 %all-to-all-start.4 = ((bf16[16,96,512]{2,1,0:T(8,128)(2,1)}), bf16[16,96,512]{2,1,0:T(8,128)(2,1)S(1)}, u32[]{:S(2)}, u32[]{:S(2)}) async-start(bf16[16,96,512]{2,1,0:T(8,128)(2,1)} %bitcast.54), calls=%async_computation.4 | async-start | bytes 3145728 | tf_op jit(solution)/shard_map/cond/branch_1_fun/all_to_all | solution.py:261
  12.0 31.6 %copy-start.8 = (s32[8]{0:T(128)S(1)}, s32[8]{0:T(128)}, u32[]{:S(2)}) copy-start(s32[8]{0:T(128)} %get-tuple-element.38) | copy-start | bytes 100 | tf_op jit(solution)/shard_map/cond
  34.8 17.6 %all-to-all-start.5 = ((bf16[4,128,512]{2,1,0:T(8,128)(2,1)}), bf16[4,128,512]{2,1,0:T(8,128)(2,1)S(1)}, u32[]{:S(2)}, u32[]{:S(2)}) async-start(bf16[4,128,512]{2,1,0:T(8,128)(2,1)} %bitcast.16), calls=%async_computation.5 | async-start | bytes 1048576 | tf_op jit(solution)/shard_map/cond/branch_1_fun/all_to_all | solution.py:261
  38.3 6.4 %collective-permute-start.4 = (bf16[3,8,512]{2,1,0:T(8,128)(2,1)S(1)}, bf16[3,8,512]{2,1,0:T(8,128)(2,1)S(1)}, u32[]{:S(2)}, u32[]{:S(2)}) collective-permute-start(bf16[3,8,512]{2,1,0:T(8,128)(2,1)S(1)} %slice_bitcast_fusion), channel_id=1, source_target_pairs={{0,16},{4,20},{8,24},{12,28},{1,17},{5,21},{9,25},{13,29},{2,18},{... | collective-permute-start | bytes 73736 | tf_op jit(solution)/shard_map/cond/branch_1_fun/ppermute | solution.py:333
  51.2 1.1 %copy-start.1 = (bf16[4,3,512,128]{3,2,1,0:T(8,128)(2,1)}, bf16[4,3,512,128]{3,2,1,0:T(8,128)(2,1)S(1)}, u32[]{:S(2)}) copy-start(bf16[4,3,512,128]{3,2,1,0:T(8,128)(2,1)S(1)} %get-tuple-element.41.mixed_ref) | copy-start | bytes 4718596 | tf_op jit(solution)/shard_map/cond
  52.4 25.3 %all-to-all-start.6 = ((bf16[4,128,512]{2,1,0:T(8,128)(2,1)}), bf16[4,128,512]{2,1,0:T(8,128)(2,1)S(1)}, u32[]{:S(2)}, u32[]{:S(2)}) async-start(bf16[4,128,512]{2,1,0:T(8,128)(2,1)} %get-tuple-element.42.att_ref), calls=%async_computation.6 | async-start | bytes 1048576 | tf_op jit(solution)/shard_map/cond/branch_1_fun/all_to_all | solution.py:261
  56.1 1.4 %copy-start.2 = (bf16[4,3,512,128]{3,2,1,0:T(8,128)(2,1)S(1)}, bf16[4,3,512,128]{3,2,1,0:T(8,128)(2,1)}, u32[]{:S(2)}) copy-start(bf16[4,3,512,128]{3,2,1,0:T(8,128)(2,1)} %copy-done.1) | copy-start | bytes 4718596 | tf_op jit(solution)/shard_map/cond
  70.2 6.9 %collective-permute-start.6 = (f32[3,8,512]{2,1,0:T(8,128)S(1)}, f32[3,8,512]{2,1,0:T(8,128)S(1)}, u32[]{:S(2)}, u32[]{:S(2)}) collective-permute-start(f32[3,8,512]{2,1,0:T(8,128)S(1)} %get-tuple-element.48), channel_id=1, source_target_pairs={{16,0},{20,4},{24,8},{28,12},{17,1},{21,5},{25,9},{29,13},{18,2},{... | collective-permute-start | bytes 147464 | tf_op jit(solution)/shard_map/cond/branch_1_fun/ppermute | solution.py:340
  77.7 34.9 %all-to-all-start.7 = ((bf16[16,96,512]{2,1,0:T(8,128)(2,1)}), bf16[16,96,512]{2,1,0:T(8,128)(2,1)S(1)}, u32[]{:S(2)}, u32[]{:S(2)}) async-start(bf16[16,96,512]{2,1,0:T(8,128)(2,1)} %bitcast.20), calls=%async_computation.7 | async-start | bytes 3145728 | tf_op jit(solution)/shard_map/cond/branch_1_fun/all_to_all | solution.py:261
  82.4 19.3 %collective-permute-start.5 = (f32[3,7,512]{2,1,0:T(8,128)S(1)}, f32[3,7,512]{2,1,0:T(8,128)S(1)}, u32[]{:S(2)}, u32[]{:S(2)}) collective-permute-start(f32[3,7,512]{2,1,0:T(8,128)S(1)} %get-tuple-element.44), channel_id=1, source_target_pairs={{0,16},{4,20},{8,24},{12,28},{16,0},{20,4},{24,8},{28,12},{1,17},{... | collective-permute-start | bytes 129032 | tf_op jit(solution)/shard_map/cond/branch_1_fun/ppermute | solution.py:273
  102.5 4.8 %collective-permute-start.7 = (f32[3,7,512]{2,1,0:T(8,128)S(1)}, f32[3,7,512]{2,1,0:T(8,128)S(1)}, u32[]{:S(2)}, u32[]{:S(2)}) collective-permute-start(f32[3,7,512]{2,1,0:T(8,128)S(1)} %add.40.refs_0_), channel_id=1, source_target_pairs={{0,4},{4,0},{8,12},{12,8},{16,20},{20,16},{24,28},{28,24},{1,5},{5... | collective-permute-start | bytes 129032 | tf_op jit(solution)/shard_map/cond/branch_1_fun/ppermute | solution.py:273
  105.2 4.1 %collective-permute-start.8 = (f32[3,7,512]{2,1,0:T(8,128)S(1)}, f32[3,7,512]{2,1,0:T(8,128)S(1)}, u32[]{:S(2)}, u32[]{:S(2)}) collective-permute-start(f32[3,7,512]{2,1,0:T(8,128)S(1)} %add.40.refs_0_), channel_id=1, source_target_pairs={{0,8},{4,12},{8,0},{12,4},{16,24},{20,28},{24,16},{28,20},{1,9},{5... | collective-permute-start | bytes 129032 | tf_op jit(solution)/shard_map/cond/branch_1_fun/ppermute | solution.py:273
  106.9 5.0 %collective-permute-start.9 = (f32[3,7,512]{2,1,0:T(8,128)S(1)}, f32[3,7,512]{2,1,0:T(8,128)S(1)}, u32[]{:S(2)}, u32[]{:S(2)}) collective-permute-start(f32[3,7,512]{2,1,0:T(8,128)S(1)} %add.40.refs_0_), channel_id=1, source_target_pairs={{0,12},{4,8},{8,4},{12,0},{16,28},{20,24},{24,20},{28,16},{1,13},{... | collective-permute-start | bytes 129032 | tf_op jit(solution)/shard_map/cond/branch_1_fun/ppermute | solution.py:273
